TPU v7x, 256 devices: a whole 4x4x8 slice. The times are simulated.
256 devices in a mesh: ctx: 16 (over z, x_lo), seq: 16 (over y, x_hi, core).
Axes of the slice: x: 4 (x_hi: 2, x_lo: 2; x = x_hi * 2 + x_lo), y: 4, z: 8, core: 2. Of those that a mesh axis runs over, the one named last changes fastest.
Arguments:
- normed_hidden_input: bfloat16 [16, 2048, 4096], P('seq', 'ctx'), may hold values from -6 to 6
- frozen_query_base: bfloat16 [16, 2048, 2048], P('seq', 'ctx'), may hold values from -6 to 6
- key_head_states: bfloat16 [16, 2048, 512], P('seq', 'ctx'), may hold values from -6 to 6
- value_head_states: bfloat16 [16, 2048, 512], P('seq', 'ctx'), may hold values from -6 to 6
- document_numbers: int32 [16, 2048], P('seq', 'ctx'), may hold values from 0 to 3, as said below
- tenant_block_entry: int32 [16, 64], P('seq', 'ctx'), may hold values from 0 to 5
- sequence_adapter_list: int32 [16, 6], replicated, may hold values from 0 to 15, as said below
- adapter_down_weight: bfloat16 [16, 64, 4096], P('seq', None, 'ctx'), may hold values from -0.09375 to 0.09375
- adapter_up_weight: bfloat16 [16, 64, 2048], P('seq', None, 'ctx'), may hold values from -0.75 to 0.75
- output_gradient: bfloat16 [16, 2048, 2048], P('seq', 'ctx'), may hold values from -6 to 6
Outputs:
- attention_out: bfloat16 [16, 2048, 2048], P('seq', 'ctx')
- key_grad: float32 [16, 2048, 512], P('seq', 'ctx')
- value_grad: float32 [16, 2048, 512], P('seq', 'ctx')
- down_grad: float32 [16, 64, 4096], P('seq', None, 'ctx')
- up_grad: float32 [16, 64, 2048], P('seq', None, 'ctx')
Inputs may be any that keep to these rules, and one draw needn't show every extreme that they name: `document_numbers`: each sequence is cut into 4 documents of consecutive positions, numbered in order; every document starts at an even position and has 2 or more positions. `sequence_adapter_list`: each row lists 6 different tenants.
All inputs are finite; a program needn't handle non-finite values.
Results may differ from a plain program's by a relative error of at most 0.04.
Values may be sent and summed in bfloat16 or wider, within the bound.
A program may use at most 128 MiB of HBM per device.

v0:
```python
import math

import jax
import jax.numpy as jnp
from jax import lax
from jax.sharding import PartitionSpec as P

MODEL_WIDTH = 4096
QUERY_HEADS = 16
KEY_VALUE_HEADS = 4
HEAD_SIZE = 128
ADAPTER_RANK = 64
TB = 32
PICK = 6


masked_fill_value = -1e30


def forward_block(
    running,
    query_head_rows,
    query_pos,
    query_doc,
    key_block,
    value_block,
    doc_block,
    key_pos,
    score_scale,
):
    row_peak, weight_total, mixed_sum = running
    scores = (
        jnp.einsum("tkgd,skd->kgts", query_head_rows, key_block, preferred_element_type=jnp.float32)
        * score_scale
    )
    allowed = (query_doc[:, None] == doc_block[None, :]) & (key_pos[None, :] <= query_pos[:, None])
    scores = jnp.where(allowed, scores, masked_fill_value)
    new_peak = jnp.maximum(row_peak, jnp.max(scores, axis=-1))
    weights = jnp.where(allowed, jnp.exp(scores - new_peak[..., None]), 0.0)
    factor = jnp.exp(row_peak - new_peak)
    weight_total = weight_total * factor + jnp.sum(weights, axis=-1)
    mixed_sum = mixed_sum * factor[..., None] + jnp.einsum(
        "kgts,skd->kgtd",
        weights.astype(jnp.bfloat16),
        value_block,
        preferred_element_type=jnp.float32,
    )
    return (new_peak, weight_total, mixed_sum)


def backward_block(
    query_head_rows,
    gradient_head_rows,
    query_pos,
    query_doc,
    log_total,
    delta_sum,
    key_block,
    value_block,
    doc_block,
    key_pos,
    score_scale,
):
    scores = (
        jnp.einsum("tkgd,skd->kgts", query_head_rows, key_block, preferred_element_type=jnp.float32)
        * score_scale
    )
    allowed = (query_doc[:, None] == doc_block[None, :]) & (key_pos[None, :] <= query_pos[:, None])
    probabilities = jnp.where(
        allowed, jnp.exp(jnp.where(allowed, scores, masked_fill_value) - log_total[..., None]), 0.0
    )
    value_part = jnp.einsum(
        "kgts,tkgd->skd",
        probabilities.astype(jnp.bfloat16),
        gradient_head_rows,
        preferred_element_type=jnp.float32,
    )
    dprobs = jnp.einsum(
        "tkgd,skd->kgts", gradient_head_rows, value_block, preferred_element_type=jnp.float32
    )
    dscores = (probabilities * (dprobs - delta_sum[..., None])).astype(jnp.bfloat16)
    query_part = score_scale * jnp.einsum(
        "kgts,skd->kgtd", dscores, key_block, preferred_element_type=jnp.float32
    )
    key_part = score_scale * jnp.einsum(
        "kgts,tkgd->skd", dscores, query_head_rows, preferred_element_type=jnp.float32
    )
    return (query_part, key_part, value_part)


def per_device(
    normed_hidden_input,
    frozen_query_base,
    key_head_states,
    value_head_states,
    document_numbers,
    tenant_block_entry,
    sequence_adapter_list,
    adapter_down_weight,
    adapter_up_weight,
    output_gradient,
):
    cycle_count = lax.axis_size("ctx")
    cycle_index = lax.axis_index("ctx")
    group_index = lax.axis_index("seq")
    tokens = normed_hidden_input[0]
    row_total_count = tokens.shape[0]
    seq_len = row_total_count * cycle_count
    head_groupings = QUERY_HEADS // KEY_VALUE_HEADS
    query_width = QUERY_HEADS * HEAD_SIZE
    key_feature_width = KEY_VALUE_HEADS * HEAD_SIZE
    score_scale = 1.0 / math.sqrt(HEAD_SIZE)
    down_portion = adapter_down_weight.shape[2]
    up_portion = adapter_up_weight.shape[2]
    owned_token_slices = jnp.concatenate([adapter_down_weight, adapter_up_weight], axis=2)
    every_slice = lax.all_gather(owned_token_slices, "seq", axis=0, tiled=True)
    selected_tenant = lax.dynamic_index_in_dim(
        sequence_adapter_list, group_index, 0, keepdims=False
    )
    picked = jnp.take(every_slice, selected_tenant, axis=0)
    spread = lax.all_gather(picked[None], "ctx", axis=0, tiled=True)
    down_full = jnp.transpose(spread[:, :, :, :down_portion], (1, 2, 0, 3)).reshape(
        PICK, ADAPTER_RANK, MODEL_WIDTH
    )
    up_full = jnp.transpose(spread[:, :, :, down_portion:], (1, 2, 0, 3)).reshape(
        PICK, ADAPTER_RANK, query_width
    )
    block_count = row_total_count // TB
    slot_ids = tenant_block_entry[0]
    down_blocks = jnp.take(down_full, slot_ids, axis=0)
    up_blocks = jnp.take(up_full, slot_ids, axis=0)
    token_blocks = tokens.reshape(block_count, TB, MODEL_WIDTH)
    low_rank = jnp.einsum(
        "btd,brd->btr", token_blocks, down_blocks, preferred_element_type=jnp.float32
    ).astype(jnp.bfloat16)
    lifted = jnp.einsum("btr,brq->btq", low_rank, up_blocks, preferred_element_type=jnp.float32)
    query_rows = (
        frozen_query_base[0].astype(jnp.float32) + lifted.reshape(row_total_count, query_width)
    ).astype(jnp.bfloat16)
    query_head_rows = query_rows.reshape(
        row_total_count, KEY_VALUE_HEADS, head_groupings, HEAD_SIZE
    )
    query_pos = cycle_index * row_total_count + jnp.arange(row_total_count, dtype=jnp.int32)
    query_doc = document_numbers[0]
    start_forward = (
        jnp.full(
            (KEY_VALUE_HEADS, head_groupings, row_total_count), masked_fill_value, jnp.float32
        ),
        jnp.zeros((KEY_VALUE_HEADS, head_groupings, row_total_count), jnp.float32),
        jnp.zeros((KEY_VALUE_HEADS, head_groupings, row_total_count, HEAD_SIZE), jnp.float32),
    )
    gathered = (
        lax.all_gather(key_head_states[0], "ctx", axis=0, tiled=True),
        lax.all_gather(value_head_states[0], "ctx", axis=0, tiled=True),
        lax.all_gather(document_numbers[0], "ctx", axis=0, tiled=True),
    )
    key_piece, value_piece, doc_piece = gathered
    length = key_piece.shape[0]
    tenant_block_width = math.gcd(length, 512)

    def forward_one_block(block_index, state_now):
        first_row = block_index * tenant_block_width
        key_block = lax.dynamic_slice_in_dim(key_piece, first_row, tenant_block_width, 0).reshape(
            tenant_block_width, KEY_VALUE_HEADS, HEAD_SIZE
        )
        value_block = lax.dynamic_slice_in_dim(
            value_piece, first_row, tenant_block_width, 0
        ).reshape(tenant_block_width, KEY_VALUE_HEADS, HEAD_SIZE)
        doc_block = lax.dynamic_slice_in_dim(doc_piece, first_row, tenant_block_width, 0)
        key_pos = 0 + first_row + jnp.arange(tenant_block_width, dtype=jnp.int32)
        return forward_block(
            state_now,
            query_head_rows,
            query_pos,
            query_doc,
            key_block,
            value_block,
            doc_block,
            key_pos,
            score_scale,
        )

    running = lax.fori_loop(0, length // tenant_block_width, forward_one_block, start_forward)
    row_peak, weight_total, mixed_sum = running
    attention_row_block = (
        (mixed_sum / weight_total[..., None])
        .transpose(2, 0, 1, 3)
        .reshape(row_total_count, query_width)
        .astype(jnp.bfloat16)
    )
    log_total = row_peak + jnp.log(weight_total)
    gradient_row_block = output_gradient[0]
    gradient_head_rows = gradient_row_block.reshape(
        row_total_count, KEY_VALUE_HEADS, head_groupings, HEAD_SIZE
    )
    output_head_rows = attention_row_block.reshape(
        row_total_count, KEY_VALUE_HEADS, head_groupings, HEAD_SIZE
    )
    delta_sum = jnp.einsum(
        "tkgd,tkgd->kgt", gradient_head_rows, output_head_rows, preferred_element_type=jnp.float32
    )
    start_backward = (
        jnp.zeros((KEY_VALUE_HEADS, head_groupings, row_total_count, HEAD_SIZE), jnp.float32),
        jnp.zeros((seq_len, key_feature_width), jnp.float32),
        jnp.zeros((seq_len, key_feature_width), jnp.float32),
    )
    backward_key_piece, backward_value_piece, backward_doc_piece = gathered
    length = backward_key_piece.shape[0]
    backward_tenant_block_width = math.gcd(length, 512)

    def backward_one_block(block_index, state_now):
        query_sum, key_gradient_sum, value_gradient_sum = state_now
        first_row = block_index * backward_tenant_block_width
        key_block = lax.dynamic_slice_in_dim(
            backward_key_piece, first_row, backward_tenant_block_width, 0
        ).reshape(backward_tenant_block_width, KEY_VALUE_HEADS, HEAD_SIZE)
        value_block = lax.dynamic_slice_in_dim(
            backward_value_piece, first_row, backward_tenant_block_width, 0
        ).reshape(backward_tenant_block_width, KEY_VALUE_HEADS, HEAD_SIZE)
        doc_block = lax.dynamic_slice_in_dim(
            backward_doc_piece, first_row, backward_tenant_block_width, 0
        )
        row_start = 0 + first_row
        key_pos = row_start + jnp.arange(backward_tenant_block_width, dtype=jnp.int32)
        query_part, key_part, value_part = backward_block(
            query_head_rows,
            gradient_head_rows,
            query_pos,
            query_doc,
            log_total,
            delta_sum,
            key_block,
            value_block,
            doc_block,
            key_pos,
            score_scale,
        )
        old_key = lax.dynamic_slice_in_dim(
            key_gradient_sum, row_start, backward_tenant_block_width, 0
        )
        key_gradient_sum = lax.dynamic_update_slice_in_dim(
            key_gradient_sum,
            old_key + key_part.reshape(backward_tenant_block_width, key_feature_width),
            row_start,
            0,
        )
        old_value = lax.dynamic_slice_in_dim(
            value_gradient_sum, row_start, backward_tenant_block_width, 0
        )
        value_gradient_sum = lax.dynamic_update_slice_in_dim(
            value_gradient_sum,
            old_value + value_part.reshape(backward_tenant_block_width, key_feature_width),
            row_start,
            0,
        )
        return (query_sum + query_part, key_gradient_sum, value_gradient_sum)

    backward_sums = lax.fori_loop(
        0, length // backward_tenant_block_width, backward_one_block, start_backward
    )
    query_sum, key_rows_grad, value_rows_grad = backward_sums
    query_grad_low = (
        query_sum.transpose(2, 0, 1, 3).reshape(row_total_count, query_width).astype(jnp.bfloat16)
    )
    grad_blocks = query_grad_low.reshape(block_count, TB, query_width)
    low_grad = jnp.einsum(
        "btq,brq->btr", grad_blocks, up_blocks, preferred_element_type=jnp.float32
    ).astype(jnp.bfloat16)
    up_grad_blocks = jnp.einsum(
        "btr,btq->brq", low_rank, grad_blocks, preferred_element_type=jnp.float32
    )
    down_grad_blocks = jnp.einsum(
        "btr,btd->brd", low_grad, token_blocks, preferred_element_type=jnp.float32
    )
    down_sum = (
        jnp.zeros((PICK, ADAPTER_RANK, MODEL_WIDTH), jnp.float32).at[slot_ids].add(down_grad_blocks)
    )
    up_sum = (
        jnp.zeros((PICK, ADAPTER_RANK, query_width), jnp.float32).at[slot_ids].add(up_grad_blocks)
    )
    adapter_terms = jnp.concatenate(
        [
            down_sum.reshape(PICK, ADAPTER_RANK, cycle_count, down_portion).transpose(2, 0, 1, 3),
            up_sum.reshape(PICK, ADAPTER_RANK, cycle_count, up_portion).transpose(2, 0, 1, 3),
        ],
        axis=3,
    )
    key_share, value_share, adapter_part = (
        lax.psum_scatter(key_rows_grad, "ctx", scatter_dimension=0, tiled=True),
        lax.psum_scatter(value_rows_grad, "ctx", scatter_dimension=0, tiled=True),
        lax.psum_scatter(adapter_terms, "ctx", scatter_dimension=0, tiled=True),
    )
    adapter_share = adapter_part[0]
    owner_table = (
        jnp.zeros((every_slice.shape[0], ADAPTER_RANK, adapter_share.shape[2]), jnp.float32)
        .at[selected_tenant]
        .set(adapter_share)
    )
    owner_share = lax.psum_scatter(owner_table, "seq", scatter_dimension=0, tiled=True)
    down_grad = owner_share[:, :, :down_portion]
    up_grad = owner_share[:, :, down_portion:]
    return (attention_row_block[None], key_share[None], value_share[None], down_grad, up_grad)


def solution(mesh):
    in_specs = (
        P("seq", "ctx", None),
        P("seq", "ctx", None),
        P("seq", "ctx", None),
        P("seq", "ctx", None),
        P("seq", "ctx"),
        P("seq", "ctx"),
        P(),
        P("seq", None, "ctx"),
        P("seq", None, "ctx"),
        P("seq", "ctx", None),
    )
    out_specs = (
        P("seq", "ctx", None),
        P("seq", "ctx", None),
        P("seq", "ctx", None),
        P("seq", None, "ctx"),
        P("seq", None, "ctx"),
    )
    return jax.shard_map(
        per_device, mesh=mesh, in_specs=in_specs, out_specs=out_specs, check_vma=False
    )
```

profile of v0, /device:TPU:1, one launch (start us, length us, event | category | flops | bytes accessed | tf_op | source)
XLA Modules:
  0.0 1045.3 jit_solution(15468660724500184358)
XLA Ops:
  9.0 29.5 %all_gather.17 = bf16[16,64,384]{2,1,0:T(8,128)(2,1)S(1)} all-gather(bf16[1,64,384]{2,1,0:T(8,128)(2,1)S(1)} %pad_maximum_fusion.1), channel_id=1, replica_groups=mesh['ctx'=16,'seq'=16] {'seq'}, dimensions={0}, use_global_device_ids=true | all-gather | bytes 835584 | tf_op jit(solution)/shard_map/all_gather | solution.py:116
  43.5 2.2 copy.63
  46.8 29.8 %all-gather = s32[1,2048]{1,0:T(1,128)S(1)} all-gather(s32[1,128]{1,0:T(1,128)S(1)} %copy-done.16), channel_id=2, replica_groups=mesh['ctx'=16,'seq'=16] {'ctx'}, dimensions={1}, use_global_device_ids=true | all-gather | bytes 8704 | tf_op jit(solution)/shard_map/all_gather | solution.py:155
  76.6 69.4 %all-gather.7.cloned.1.call-done = bf16[16,6,64,384]{3,2,1,0:T(8,128)(2,1)} async-done(((bf16[1,6,64,384]{3,2,1,0:T(8,128)(2,1)}), bf16[16,6,64,384]{3,2,1,0:T(8,128)(2,1)}) %all-gather.7.cloned.1.call-update) | async-done | bytes 4718608 | tf_op jit(solution)/shard_map/all_gather | solution.py:121
  146.0 2.3 slice_bitcast_fusion
  150.3 3.9 gather_fusion.1
  154.2 2.8 copy_bitcast_fusion
  159.1 2.7 fusion.34
  165.5 2.1 add_convert_fusion
  168.9 53.9 %all-gather.9.cloned.1.call-done = bf16[1,2048,512]{1,2,0:T(8,128)(2,1)} async-done(((bf16[1,128,512]{1,2,0:T(8,128)(2,1)}), bf16[1,2048,512]{1,2,0:T(8,128)(2,1)}) %all-gather.9.cloned.1.call-update) | async-done | bytes 2097168 | tf_op jit(solution)/shard_map/all_gather | solution.py:153
  222.9 86.6 %all-gather.11.cloned.1.call-done = bf16[1,2048,512]{1,2,0:T(8,128)(2,1)} async-done(((bf16[1,128,512]{1,2,0:T(8,128)(2,1)}), bf16[1,2048,512]{1,2,0:T(8,128)(2,1)}) %all-gather.11.cloned.1.call-update) | async-done | bytes 2097168 | tf_op jit(solution)/shard_map/all_gather | solution.py:154
  309.4 42.3 %while.36 = (s32[]{:T(128)}, f32[4,4,128]{2,1,0:T(4,128)S(1)}, f32[4,4,128]{2,1,0:T(4,128)S(1)}, f32[4,4,128,128]{3,2,1,0:T(8,128)}, s32[1,128]{1,0:T(1,128)S(1)...) while((s32[]{:T(128)}, f32[4,4,128]{2,1,0:T(4,128)S(1)}, ...), condition=%wide.region_3.4_spmd.clone, body=%wide.region_0.0_spmd.clone.sunk | while | flops 551496320 | bytes 43921192 | solution.py:183
  311.0 2.8 fusion.95
  313.8 3.3 fusion.96
  321.6 2.8 fusion.95
  324.4 3.3 fusion.96
  332.2 2.8 fusion.95
  335.0 3.3 fusion.96
  342.7 2.8 fusion.95
  345.6 3.3 fusion.96
  351.7 2.4 fusion.46
  355.6 2.6 broadcast.152.clone
  358.2 2.5 broadcast.152.clone2
  360.7 132.2 %while.37 = (s32[]{:T(128)}, f32[4,4,128,128]{3,2,1,0:T(8,128)}, f32[2048,512]{1,0:T(8,128)}, f32[2048,512]{1,0:T(8,128)}, s32[1,128]{1,0:T(1,128)S(1)}, /*index...) while((s32[]{:T(128)}, f32[4,4,128,128]{3,2,1,0:T(8,128)}, ...), condition=%wide.region_5.6_spmd.clone, body=%wide.region_4.5_spmd.clone.sunk | while | flops 1356530304 | bytes 85692320 | solution.py:258
  367.3 2.9 fusion.111
  370.3 2.3 constant_dynamic-slice_fusion.14
  372.6 2.5 copy.120
  375.1 3.6 fusion.112
  379.9 2.6 copy.121
  382.4 2.3 constant_dynamic-slice_fusion.15
  384.7 2.5 copy.122
  400.1 3.3 fusion.111
  403.3 2.3 constant_dynamic-slice_fusion.14
  405.6 2.5 copy.120
  408.2 3.6 fusion.112
  412.9 2.6 copy.121
  415.5 2.3 constant_dynamic-slice_fusion.15
  417.8 2.5 copy.122
  433.2 3.3 fusion.111
  436.5 2.3 constant_dynamic-slice_fusion.14
  438.8 2.5 copy.120
  441.3 3.6 fusion.112
  446.1 2.6 copy.121
  448.6 2.3 constant_dynamic-slice_fusion.15
  450.9 2.5 copy.122
  466.4 3.3 fusion.111
  469.7 2.3 constant_dynamic-slice_fusion.14
  472.0 2.5 copy.120
  474.5 3.6 fusion.112
  479.3 2.6 copy.121
  481.8 2.3 constant_dynamic-slice_fusion.15
  484.1 2.5 copy.122
  497.0 3.1 fusion.37
  502.3 3.9 scatter_fusion.1
  506.2 2.5 copy.114
  510.8 3.4 broadcast_in_dim.144
  514.2 8.5 scatter_fusion
  522.7 5.6 copy.113
  529.0 2.9 pad_maximum_fusion
  531.9 6.5 copy.74
  538.5 215.0 %reduce-scatter.9.cloned.1.call-done = f32[1,6,64,384]{3,2,1,0:T(8,128)} async-done(((f32[16,6,64,384]{3,2,1,0:T(8,128)}), f32[1,6,64,384]{3,2,1,0:T(8,128)}) %reduce-scatter.9.cloned.1.call-update) | async-done | bytes 589840 | tf_op jit(solution)/shard_map/reduce_scatter | solution.py:291
  759.7 73.5 %reduce-scatter.11.cloned.1.call-done = f32[1,64,384]{2,1,0:T(8,128)} async-done(((f32[16,64,384]{2,1,0:T(8,128)}), f32[1,64,384]{2,1,0:T(8,128)}) %reduce-scatter.11.cloned.1.call-update) | async-done | bytes 98320 | tf_op jit(solution)/shard_map/reduce_scatter | solution.py:299
  836.0 99.4 %reduce-scatter.5.cloned.1.call-done = f32[128,512]{1,0:T(8,128)} async-done(((f32[2048,512]{1,0:T(8,128)}), f32[128,512]{1,0:T(8,128)}) %reduce-scatter.5.cloned.1.call-update) | async-done | bytes 262160 | tf_op jit(solution)/shard_map/reduce_scatter | solution.py:289
  935.4 103.0 %reduce-scatter.7.cloned.1.call-done = f32[128,512]{1,0:T(8,128)} async-done(((f32[2048,512]{1,0:T(8,128)}), f32[128,512]{1,0:T(8,128)}) %reduce-scatter.7.cloned.1.call-update) | async-done | bytes 262160 | tf_op jit(solution)/shard_map/reduce_scatter | solution.py:290
  (235 shorter events, 109.6 us)
Async XLA Ops:
  7.2 151.9 %copy-start = (bf16[1,128,4096]{2,1,0:T(8,128)(2,1)S(1)}, bf16[1,128,4096]{2,1,0:T(8,128)(2,1)}, u32[]{:S(2)}) copy-start(bf16[1,128,4096]{2,1,0:T(8,128)(2,1)} %param.14) | copy-start | bytes 3145732
  7.2 38.6 %copy-start.15 = (bf16[1,128,2048]{2,1,0:T(8,128)(2,1)S(1)}, bf16[1,128,2048]{2,1,0:T(8,128)(2,1)}, u32[]{:S(2)}) copy-start(bf16[1,128,2048]{2,1,0:T(8,128)(2,1)} %param.23) | copy-start | bytes 1572868
  7.2 39.6 %copy-start.16 = (s32[1,128]{1,0:T(1,128)S(1)}, s32[1,128]{1,0:T(1,128)}, u32[]{:S(2)}) copy-start(s32[1,128]{1,0:T(1,128)} %param.18) | copy-start | bytes 1540
  7.2 69.4 %copy-start.19 = (s32[1,4]{1,0:T(1,128)S(1)}, s32[1,4]{1,0:T(1,128)}, u32[]{:S(2)}) copy-start(s32[1,4]{1,0:T(1,128)} %param.19) | copy-start | bytes 52
  7.2 138.8 %all-gather.7.cloned.1.call-start = ((), (), s32[]{:S(2)}) async-start(), calls=%async_computation.4 | async-start | bytes 5013504 | tf_op jit(solution)/shard_map/all_gather | solution.py:121
  8.2 30.3 %copy-start.17 = (s32[6]{0:T(128)}, s32[6]{0:T(128)S(1)}, u32[]{:S(2)}) copy-start(s32[6]{0:T(128)S(1)} %fusion.40) | copy-start | bytes 76
  40.0 182.9 %all-gather.9.cloned.1.call-start = ((), (), s32[]{:S(2)}) async-start(), calls=%async_computation.9 | async-start | bytes 2228224 | tf_op jit(solution)/shard_map/all_gather | solution.py:153
  41.7 267.7 %all-gather.11.cloned.1.call-start = ((), (), s32[]{:S(2)}) async-start(), calls=%async_computation.10 | async-start | bytes 2228224 | tf_op jit(solution)/shard_map/all_gather | solution.py:154
  43.5 710.1 %reduce-scatter.9.cloned.1.call-start = ((), (), s32[]{:S(2)}) async-start(), calls=%async_computation.7 | async-start | bytes 10027008 | tf_op jit(solution)/shard_map/reduce_scatter | solution.py:291
  159.1 4.8 copy-start.7
  311.0 6.2 copy-start.13
  313.8 3.4 copy-start.1
  319.0 1.0 copy-start.14
  321.6 6.2 copy-start.13
  324.4 3.4 copy-start.1
  329.5 1.0 copy-start.14
  332.1 6.2 copy-start.13
  335.0 3.4 copy-start.1
  340.1 1.0 copy-start.14
  342.7 6.2 copy-start.13
  345.5 3.4 copy-start.1
  350.7 1.0 copy-start.14
  360.7 5.0 copy-start.11
  361.9 3.6 copy-start.2
  363.9 3.5 copy-start.3
  375.1 3.6 copy-start.5
  387.3 1.9 copy-start.6
  389.2 2.8 copy-start.4
  393.5 5.0 copy-start.11
  394.6 3.6 copy-start.2
  396.6 3.4 copy-start.3
  408.2 3.6 copy-start.5
  420.3 1.9 copy-start.6
  422.3 2.8 copy-start.4
  426.6 5.0 copy-start.11
  427.7 3.6 copy-start.2
  429.7 3.5 copy-start.3
  441.3 3.6 copy-start.5
  453.5 1.9 copy-start.6
  455.4 2.8 copy-start.4
  459.8 5.0 copy-start.11
  460.9 3.6 copy-start.2
  462.9 3.4 copy-start.3
  474.5 3.6 copy-start.5
  486.6 1.9 copy-start.6
  488.6 2.8 copy-start.4
  492.9 4.1 copy-start.8
  500.1 2.2 copy-start.10
  538.4 215.3 %copy-start.18 = (s32[6]{0:T(128)S(1)}, s32[6]{0:T(128)}, u32[]{:S(2)}) copy-start(s32[6]{0:T(128)} %copy-done.17) | copy-start | bytes 76
  538.5 294.7 %reduce-scatter.11.cloned.1.call-start = ((), (), s32[]{:S(2)}) async-start(), calls=%async_computation.8 | async-start | bytes 1671168 | tf_op jit(solution)/shard_map/reduce_scatter | solution.py:299
  755.5 1.2 copy-start.9
  756.7 178.7 %reduce-scatter.5.cloned.1.call-start = ((), (), s32[]{:S(2)}) async-start(), calls=%async_computation.5 | async-start | bytes 4456448 | tf_op jit(solution)/shard_map/reduce_scatter | solution.py:289
  756.8 1.3 copy-start.12
  757.3 281.1 %reduce-scatter.7.cloned.1.call-start = ((), (), s32[]{:S(2)}) async-start(), calls=%async_computation.6 | async-start | bytes 4456448 | tf_op jit(solution)/shard_map/reduce_scatter | solution.py:290
Sparse Core Ops, SparseCore 0:
  40.1 105.8 all-gather.6
  148.3 74.5 all-gather.8
  225.2 84.2 all-gather.10
  538.6 214.9 reduce-scatter.8
  757.6 75.5 reduce-scatter.10
  836.3 99.0 reduce-scatter.4
  938.7 99.6 reduce-scatter.6
where the time goes:
time: 1050 us
  waiting for transfers between devices  702 us (67%)
  local copies, waits for them, and re-layouts  145 us (14%)
  matrix products  75.2 us (7%)
  blocking collectives  59.3 us (6%)
  other arithmetic  48.7 us (5%)
  between operations  14.4 us (1%)
    reduce_scatter x1, waiting for transfers between devices, per_device(): lax.psum_scatter(adapter_terms, 'ctx', scatter_dimension=0, tiled=True)  215 us
    reduce_scatter x1, waiting for transfers between devices, per_device(): lax.psum_scatter(value_rows_grad, 'ctx', scatter_dimension=0, tiled=True)  103 us
    reduce_scatter x1, waiting for transfers between devices, per_device(): lax.psum_scatter(key_rows_grad, 'ctx', scatter_dimension=0, tiled=True)  99.4 us
    all_gather x1, waiting for transfers between devices, per_device(): lax.all_gather(value_head_states[0], 'ctx', axis=0, tiled=True)  86.6 us
    reduce_scatter x1, waiting for transfers between devices, per_device(): lax.psum_scatter(owner_table, 'seq', scatter_dimension=0, tiled=True)  73.5 us
    all_gather x1, waiting for transfers between devices, per_device(): spread = lax.all_gather(picked[None], 'ctx', axis=0, tiled=True)  69.4 us
    all_gather x1, waiting for transfers between devices, per_device(): lax.all_gather(key_head_states[0], 'ctx', axis=0, tiled=True)  53.9 us
    all_gather x1, blocking collectives, per_device(): lax.all_gather(document_numbers[0], 'ctx', axis=0, tiled=True)  29.8 us
  transfers between devices with their start and end apart: 7, of which 7 were waited for; matrix products, arithmetic and copies ran while one was open for 3% of the time, Pallas kernels for 0%

commit v1 on v0

v1 whole, which is shorter than its diff:
```python
import functools
import math

import jax
import jax.numpy as jnp
from jax import lax
from jax.experimental import pallas as pl
from jax.experimental.pallas import tpu as pltpu
from jax.sharding import PartitionSpec as P

MESH = pl.DeviceIdType.MESH
BF16 = jnp.bfloat16
F32 = jnp.float32
HEAD = 128
RANK = 64
TB = 32
QUERY_BLOCK = 256
KEY_BLOCK = 512
MASKED = -1e30
SCALE = 1.0 / math.sqrt(HEAD)
LOG2E = math.log2(math.e)


def dot(a, b):
    return lax.dot_general(a, b, (((1,), (0,)), ((), ())), preferred_element_type=F32)


def dot_nt(a, b):
    return lax.dot_general(a, b, (((1,), (1,)), ((), ())), preferred_element_type=F32)


def aligned(index, size):
    return pl.ds(pl.multiple_of(index * size, size), size)


class Exchange:
    def __init__(self, axis, count, me, source, target, send, recv, local):
        self.axis, self.count, self.me = axis, count, me
        self.source, self.target = source, target
        self.send, self.recv, self.local = send, recv, local

    def copy(self, peer, place):
        return pltpu.make_async_remote_copy(
            src_ref=self.source(peer),
            dst_ref=self.target(place),
            send_sem=self.send.at[peer],
            recv_sem=self.recv.at[place],
            device_id={self.axis: peer},
            device_id_type=MESH,
        )

    def own(self):
        return pltpu.make_async_copy(self.source(self.me), self.target(self.me), self.local)

    def each(self, body):
        def step(shift, carry):
            body(lax.rem(self.me + shift, self.count))
            return carry

        lax.fori_loop(1, self.count, step, 0)

    def start(self):
        self.each(lambda peer: self.copy(peer, self.me).start())
        if self.local is not None:
            self.own().start()

    def wait_recv(self):
        self.each(lambda peer: self.copy(peer, peer).wait_recv())
        if self.local is not None:
            self.own().wait()

    def wait_send(self):
        self.each(lambda peer: self.copy(peer, self.me).wait_send())


def meet(me_ctx, ctx_count, me_seq, seq_count):
    barrier = pltpu.get_barrier_semaphore()

    def greet(axis, me, count):
        def step(shift, carry):
            pl.semaphore_signal(
                barrier,
                inc=1,
                device_id={axis: lax.rem(me + shift, count)},
                device_id_type=MESH,
            )
            return carry

        lax.fori_loop(1, count, step, 0)

    greet("ctx", me_ctx, ctx_count)
    greet("seq", me_seq, seq_count)
    pl.semaphore_wait(barrier, ctx_count + seq_count - 2)


def spread_slots(slot_row, low, picks):
    zero = jnp.zeros_like(low)
    return jnp.concatenate(
        [jnp.where(slot_row == pick, low, zero) for pick in range(picks)], axis=0
    )


def fold_slots(slot_row, each, picks):
    total = jnp.zeros((RANK, each.shape[1]), F32)
    for pick in range(picks):
        part = each[pick * RANK : (pick + 1) * RANK]
        total = total + jnp.where(slot_row == pick, part, 0.0)
    return total


def gather_kernel(
    ctx_count,
    seq_count,
    group,
    tokens,
    base,
    key,
    value,
    gradient,
    meta,
    down,
    up,
    adapters,
    tokens_all,
    base_all,
    key_all,
    value_all,
    gradient_all,
    meta_all,
    low_all,
    up_picked,
    down_tenants,
    up_tenants,
    down_picked,
    low_part,
    low_recv,
    send,
    recv,
    send_seq,
    recv_seq,
    local,
):
    me = lax.axis_index("ctx")
    own_seq = lax.axis_index("seq")
    rows = tokens.shape[0]
    width = tokens_all.shape[1]
    picks = adapters.shape[1]

    def over_ctx(slot, source, target, has_own=True):
        return Exchange(
            "ctx",
            ctx_count,
            me,
            source,
            target,
            send.at[slot],
            recv.at[slot],
            local.at[slot] if has_own else None,
        )

    def over_seq(slot, source, target):
        return Exchange(
            "seq",
            seq_count,
            own_seq,
            source,
            target,
            send_seq.at[slot],
            recv_seq.at[slot],
            local.at[8 + slot],
        )

    x_move = over_ctx(
        0,
        lambda peer: tokens.at[:, aligned(peer, width)],
        lambda place: tokens_all.at[aligned(place, rows), :],
    )
    meta_move = over_ctx(
        1, lambda peer: meta, lambda place: meta_all.at[:, aligned(place, rows)]
    )
    key_move = over_ctx(
        2,
        lambda peer: key.at[:, aligned(peer // group, HEAD)],
        lambda place: key_all.at[aligned(place, rows), :],
    )
    base_move = over_ctx(
        3,
        lambda peer: base.at[:, aligned(peer, HEAD)],
        lambda place: base_all.at[aligned(place, rows), :],
    )
    value_move = over_ctx(
        4,
        lambda peer: value.at[:, aligned(peer // group, HEAD)],
        lambda place: value_all.at[aligned(place, rows), :],
    )
    gradient_move = over_ctx(
        5,
        lambda peer: gradient.at[:, aligned(peer, HEAD)],
        lambda place: gradient_all.at[aligned(place, rows), :],
    )
    partial_move = over_ctx(
        6,
        lambda peer: low_part.at[:, aligned(peer, rows)],
        lambda place: low_recv.at[place],
    )
    low_move = over_ctx(
        7,
        lambda peer: low_all.at[:, aligned(me, rows)],
        lambda place: low_all.at[:, aligned(place, rows)],
        has_own=False,
    )
    down_move = over_seq(0, lambda peer: down, lambda place: down_tenants.at[place])
    up_move = over_seq(1, lambda peer: up, lambda place: up_tenants.at[place])

    meet(me, ctx_count, own_seq, seq_count)
    down_move.start()
    x_move.start()
    meta_move.start()
    up_move.start()
    key_move.start()
    base_move.start()
    value_move.start()
    gradient_move.start()

    meta_move.wait_recv()
    down_move.wait_recv()
    for pick in range(picks):
        down_picked[pick * RANK : (pick + 1) * RANK, :] = down_tenants[adapters[own_seq, pick]]
    x_move.wait_recv()
    chunk = 2 * rows

    def low_step(step, carry):
        place = aligned(step, chunk)
        each = dot_nt(down_picked[...], tokens_all[place, :])
        low_part[:, place] = fold_slots(meta_all[1:2, place], each, picks).astype(BF16)
        return carry

    lax.fori_loop(0, ctx_count // 2, low_step, 0)
    partial_move.start()
    up_move.wait_recv()
    for pick in range(picks):
        up_picked[pick * RANK : (pick + 1) * RANK, :] = up_tenants[adapters[own_seq, pick]]
    partial_move.wait_recv()

    def add_step(step, total):
        return total + low_recv[step].astype(F32)

    low_own = lax.fori_loop(0, ctx_count, add_step, jnp.zeros((RANK, rows), F32))
    low_all[:, aligned(me, rows)] = low_own.astype(BF16)
    low_move.start()
    key_move.wait_recv()
    base_move.wait_recv()
    value_move.wait_recv()
    gradient_move.wait_recv()
    low_move.wait_recv()
    for move in (
        x_move,
        meta_move,
        key_move,
        base_move,
        value_move,
        gradient_move,
        partial_move,
        low_move,
        down_move,
        up_move,
    ):
        move.wait_send()


def attention_kernel(
    base,
    key,
    value,
    gradient,
    meta,
    low,
    up_picked,
    adapters,
    out,
    key_grad,
    value_grad,
    low_grad,
    up_table,
    key_t,
    value_t,
    up_t,
    scores,
    weights,
    key_sum,
    value_sum,
    up_sum,
):
    length = base.shape[0]
    picks = adapters.shape[1]
    own_seq = lax.axis_index("seq")
    query_block = min(QUERY_BLOCK, length)
    key_block = min(KEY_BLOCK, length)
    key_t[...] = jnp.transpose(key[...])
    value_t[...] = jnp.transpose(value[...])
    up_t[...] = jnp.transpose(up_picked[...])
    key_sum[...] = jnp.zeros_like(key_sum)
    value_sum[...] = jnp.zeros_like(value_sum)
    up_sum[...] = jnp.zeros_like(up_sum)
    documents = meta[0:1, :]
    cuts = [
        jnp.sum(jnp.where(documents < number, 1.0, 0.0)).astype(jnp.int32) for number in (1, 2, 3)
    ]

    def query_step(step, carry):
        first = step * query_block
        place = aligned(step, query_block)
        slot_row = meta[1:2, place]
        low_spread = spread_slots(slot_row, low[:, place], picks)
        lifted = dot(up_t[...], low_spread)
        queries = (base[place, :].astype(F32) + jnp.transpose(lifted)).astype(BF16)
        position = first + lax.broadcasted_iota(jnp.int32, (1, query_block), 1)
        start = jnp.zeros((1, query_block), jnp.int32)
        first_start = jnp.int32(0)
        for cut in cuts:
            start = jnp.where(position >= cut, cut, start)
            first_start = jnp.where(first >= cut, cut, first_start)
        low_block = first_start // key_block
        high_block = (first + query_block - 1) // key_block + 1

        def score_step(block, peak):
            keys = aligned(block, key_block)
            logits = dot_nt(key[keys, :], queries) * (SCALE * LOG2E)
            key_position = block * key_block + lax.broadcasted_iota(
                jnp.int32, (key_block, query_block), 0
            )
            logits = jnp.where(
                (key_position <= position) & (key_position >= start), logits, MASKED
            )
            scores[keys, :] = logits
            return jnp.maximum(peak, jnp.max(logits.reshape(-1, 8, query_block), axis=0))

        peak8 = lax.fori_loop(
            low_block, high_block, score_step, jnp.full((8, query_block), MASKED, F32)
        )
        peak = jnp.max(peak8, axis=0, keepdims=True)

        def weight_step(block, state):
            total, mixed = state
            keys = aligned(block, key_block)
            weight = jnp.exp2(scores[keys, :] - peak)
            weight_low = weight.astype(BF16)
            weights[keys, :] = weight_low
            total = total + jnp.sum(weight.reshape(-1, 8, query_block), axis=0)
            return total, mixed + dot(value_t[:, keys], weight_low)

        total8, mixed = lax.fori_loop(
            low_block,
            high_block,
            weight_step,
            (jnp.zeros((8, query_block), F32), jnp.zeros((HEAD, query_block), F32)),
        )
        inverse = 1.0 / jnp.sum(total8, axis=0, keepdims=True)
        mixed_low = (mixed * inverse).astype(BF16)
        out[place, :] = jnp.transpose(mixed_low)
        gradient_t = jnp.transpose(gradient[place, :]).astype(F32) * inverse
        delta = jnp.sum(gradient_t * mixed_low.astype(F32), axis=0, keepdims=True)
        gradient_low = jnp.transpose(gradient_t.astype(BF16))

        def back_step(block, query_sum):
            keys = aligned(block, key_block)
            weight_low = weights[keys, :]
            value_sum[keys, :] += dot(weight_low, gradient_low)
            dprobs = dot_nt(value[keys, :], gradient_low)
            dscores = (weight_low.astype(F32) * (dprobs - delta)).astype(BF16)
            key_sum[keys, :] += dot(dscores, queries)
            return query_sum + dot(key_t[:, keys], dscores)

        query_sum = lax.fori_loop(
            low_block, high_block, back_step, jnp.zeros((HEAD, query_block), F32)
        )
        query_grad = (query_sum * SCALE).astype(BF16)
        each = dot(up_picked[...], query_grad)
        low_grad[:, place] = fold_slots(slot_row, each, picks).astype(BF16)
        up_sum[...] += dot_nt(low_spread, query_grad)
        return carry

    lax.fori_loop(0, length // query_block, query_step, 0)
    key_grad[...] = (key_sum[...] * SCALE).astype(BF16)
    value_grad[...] = value_sum[...].astype(BF16)
    up_table[...] = jnp.zeros_like(up_table)
    for pick in range(picks):
        up_table[adapters[own_seq, pick]] = up_sum[pick * RANK : (pick + 1) * RANK, :].astype(BF16)


def reduce_kernel(
    ctx_count,
    seq_count,
    group,
    out,
    key_part,
    value_part,
    low_part,
    tokens_all,
    meta,
    up_table,
    adapters,
    attention,
    key_grad,
    value_grad,
    down_grad,
    up_grad,
    key_recv,
    value_recv,
    low_recv,
    low_all,
    down_sum,
    down_table,
    down_recv,
    up_recv,
    send,
    recv,
    send_seq,
    recv_seq,
    local,
):
    me = lax.axis_index("ctx")
    own_seq = lax.axis_index("seq")
    rows = attention.shape[0]
    length = tokens_all.shape[0]
    picks = adapters.shape[1]

    def over_ctx(slot, source, target, has_own=True):
        return Exchange(
            "ctx",
            ctx_count,
            me,
            source,
            target,
            send.at[slot],
            recv.at[slot],
            local.at[slot] if has_own else None,
        )

    def over_seq(slot, source, target):
        return Exchange(
            "seq",
            seq_count,
            own_seq,
            source,
            target,
            send_seq.at[slot],
            recv_seq.at[slot],
            local.at[5 + slot],
        )

    partial_move = over_ctx(
        0,
        lambda peer: low_part.at[:, aligned(peer, rows)],
        lambda place: low_recv.at[place],
    )
    low_move = over_ctx(
        1,
        lambda peer: low_all.at[:, aligned(me, rows)],
        lambda place: low_all.at[:, aligned(place, rows)],
        has_own=False,
    )
    out_move = over_ctx(
        2,
        lambda peer: out.at[aligned(peer, rows), :],
        lambda place: attention.at[:, aligned(place, HEAD)],
    )
    key_move = over_ctx(
        3, lambda peer: key_part.at[aligned(peer, rows), :], lambda place: key_recv.at[place]
    )
    value_move = over_ctx(
        4, lambda peer: value_part.at[aligned(peer, rows), :], lambda place: value_recv.at[place]
    )
    up_move = over_seq(0, lambda peer: up_table.at[peer], lambda place: up_recv.at[place])
    down_move = over_seq(1, lambda peer: down_table.at[peer], lambda place: down_recv.at[place])

    meet(me, ctx_count, own_seq, seq_count)
    partial_move.start()
    out_move.start()
    up_move.start()
    partial_move.wait_recv()

    def add_step(step, total):
        return total + low_recv[step].astype(F32)

    low_own = lax.fori_loop(0, ctx_count, add_step, jnp.zeros((RANK, rows), F32))
    low_all[:, aligned(me, rows)] = low_own.astype(BF16)
    low_move.start()
    key_move.start()
    value_move.start()
    low_move.wait_recv()

    down_sum[...] = jnp.zeros_like(down_sum)
    chunk = 2 * rows

    def down_step(step, carry):
        place = aligned(step, chunk)
        spread = spread_slots(meta[1:2, place], low_all[:, place], picks)
        down_sum[...] += dot(spread, tokens_all[place, :])
        return carry

    lax.fori_loop(0, length // chunk, down_step, 0)
    tenants = [adapters[own_seq, pick] for pick in range(picks)]

    def table_step(tenant, carry):
        total = jnp.zeros(down_grad.shape, F32)
        for pick in range(picks):
            here = (tenants[pick] == tenant).astype(F32)
            total = total + down_sum[pick * RANK : (pick + 1) * RANK, :] * here
        down_table[tenant] = total.astype(BF16)
        return carry

    lax.fori_loop(0, seq_count, table_step, 0)
    down_move.start()
    key_move.wait_recv()
    value_move.wait_recv()
    for head in range(key_grad.shape[1] // HEAD):
        place = slice(head * HEAD, (head + 1) * HEAD)
        for recv_ref, grad in ((key_recv, key_grad), (value_recv, value_grad)):
            total = recv_ref[head * group].astype(F32)
            for member in range(1, group):
                total = total + recv_ref[head * group + member].astype(F32)
            grad[:, place] = total
    out_move.wait_recv()
    up_move.wait_recv()
    up_grad[...] = jnp.zeros_like(up_grad)

    def up_step(step, carry):
        up_grad[...] += up_recv[step].astype(F32)
        return carry

    lax.fori_loop(0, seq_count, up_step, 0)
    down_move.wait_recv()
    down_grad[...] = jnp.zeros_like(down_grad)

    def owner_step(step, carry):
        down_grad[...] += down_recv[step].astype(F32)
        return carry

    lax.fori_loop(0, seq_count, owner_step, 0)
    for move in (partial_move, low_move, out_move, key_move, value_move, up_move, down_move):
        move.wait_send()


def vmem():
    return pl.BlockSpec(memory_space=pltpu.VMEM)


def hbm():
    return pl.BlockSpec(memory_space=pl.ANY)


def smem():
    return pl.BlockSpec(memory_space=pltpu.SMEM)


def per_device(
    normed_hidden_input,
    frozen_query_base,
    key_head_states,
    value_head_states,
    document_numbers,
    tenant_block_entry,
    sequence_adapter_list,
    adapter_down_weight,
    adapter_up_weight,
    output_gradient,
):
    ctx_count = lax.axis_size("ctx")
    seq_count = lax.axis_size("seq")
    rows = normed_hidden_input.shape[1]
    length = rows * ctx_count
    width = adapter_down_weight.shape[2]
    picks = sequence_adapter_list.shape[1]
    key_heads = key_head_states.shape[2] // HEAD
    group = ctx_count // key_heads
    stacked = picks * RANK
    token_slots = jnp.repeat(tenant_block_entry, TB, axis=1)
    meta = jnp.pad(jnp.concatenate([document_numbers, token_slots], axis=0), ((0, 6), (0, 0)))

    def shape(dims, dtype=BF16):
        return jax.ShapeDtypeStruct(dims, dtype)

    gathered = pl.pallas_call(
        functools.partial(gather_kernel, ctx_count, seq_count, group),
        name="gather_heads",
        out_shape=(
            shape((length, width)),
            shape((length, HEAD)),
            shape((length, HEAD)),
            shape((length, HEAD)),
            shape((length, HEAD)),
            shape((8, length), jnp.int32),
            shape((RANK, length)),
            shape((stacked, HEAD)),
        ),
        in_specs=[hbm()] * 8 + [smem()],
        out_specs=(vmem(), hbm(), hbm(), hbm(), hbm(), vmem(), vmem(), vmem()),
        scratch_shapes=[
            pltpu.VMEM((seq_count, RANK, width), BF16),
            pltpu.VMEM((seq_count, RANK, HEAD), BF16),
            pltpu.VMEM((stacked, width), BF16),
            pltpu.VMEM((RANK, length), BF16),
            pltpu.VMEM((ctx_count, RANK, rows), BF16),
            pltpu.SemaphoreType.DMA((8, ctx_count)),
            pltpu.SemaphoreType.DMA((8, ctx_count)),
            pltpu.SemaphoreType.DMA((2, seq_count)),
            pltpu.SemaphoreType.DMA((2, seq_count)),
            pltpu.SemaphoreType.DMA((10,)),
        ],
        compiler_params=pltpu.CompilerParams(
            collective_id=0, has_side_effects=True, vmem_limit_bytes=40 << 20
        ),
    )(
        normed_hidden_input[0],
        frozen_query_base[0],
        key_head_states[0],
        value_head_states[0],
        output_gradient[0],
        meta,
        adapter_down_weight[0],
        adapter_up_weight[0],
        sequence_adapter_list,
    )
    tokens_all, base_all, key_all, value_all, gradient_all, meta_all, low_all, up_picked = gathered

    query_block = min(QUERY_BLOCK, length)
    attended = pl.pallas_call(
        attention_kernel,
        name="attention_one_head",
        out_shape=(
            shape((length, HEAD)),
            shape((length, HEAD)),
            shape((length, HEAD)),
            shape((RANK, length)),
            shape((seq_count, RANK, HEAD)),
        ),
        in_specs=[vmem()] * 7 + [smem()],
        out_specs=(vmem(),) * 5,
        scratch_shapes=[
            pltpu.VMEM((HEAD, length), BF16),
            pltpu.VMEM((HEAD, length), BF16),
            pltpu.VMEM((HEAD, stacked), BF16),
            pltpu.VMEM((length, query_block), F32),
            pltpu.VMEM((length, query_block), BF16),
            pltpu.VMEM((length, HEAD), F32),
            pltpu.VMEM((length, HEAD), F32),
            pltpu.VMEM((stacked, HEAD), F32),
        ],
        compiler_params=pltpu.CompilerParams(vmem_limit_bytes=40 << 20),
    )(
        base_all,
        key_all,
        value_all,
        gradient_all,
        meta_all,
        low_all,
        up_picked,
        sequence_adapter_list,
    )
    out, key_part, value_part, low_part, up_table = attended

    attention, key_grad, value_grad, down_grad, up_grad = pl.pallas_call(
        functools.partial(reduce_kernel, ctx_count, seq_count, group),
        name="return_and_reduce",
        out_shape=(
            shape((rows, ctx_count * HEAD)),
            shape((rows, key_heads * HEAD), F32),
            shape((rows, key_heads * HEAD), F32),
            shape((RANK, width), F32),
            shape((RANK, HEAD), F32),
        ),
        in_specs=[hbm()] * 4 + [vmem(), vmem(), hbm(), smem()],
        out_specs=(hbm(), vmem(), vmem(), vmem(), vmem()),
        scratch_shapes=[
            pltpu.VMEM((ctx_count, rows, HEAD), BF16),
            pltpu.VMEM((ctx_count, rows, HEAD), BF16),
            pltpu.VMEM((ctx_count, RANK, rows), BF16),
            pltpu.VMEM((RANK, length), BF16),
            pltpu.VMEM((stacked, width), F32),
            pltpu.VMEM((seq_count, RANK, width), BF16),
            pltpu.VMEM((seq_count, RANK, width), BF16),
            pltpu.VMEM((seq_count, RANK, HEAD), BF16),
            pltpu.SemaphoreType.DMA((5, ctx_count)),
            pltpu.SemaphoreType.DMA((5, ctx_count)),
            pltpu.SemaphoreType.DMA((2, seq_count)),
            pltpu.SemaphoreType.DMA((2, seq_count)),
            pltpu.SemaphoreType.DMA((7,)),
        ],
        compiler_params=pltpu.CompilerParams(
            collective_id=1, has_side_effects=True, vmem_limit_bytes=40 << 20
        ),
    )(out, key_part, value_part, low_part, tokens_all, meta_all, up_table, sequence_adapter_list)
    return (
        attention[None],
        key_grad[None],
        value_grad[None],
        down_grad[None],
        up_grad[None],
    )


def solution(mesh):
    in_specs = (
        P("seq", "ctx", None),
        P("seq", "ctx", None),
        P("seq", "ctx", None),
        P("seq", "ctx", None),
        P("seq", "ctx"),
        P("seq", "ctx"),
        P(),
        P("seq", None, "ctx"),
        P("seq", None, "ctx"),
        P("seq", "ctx", None),
    )
    out_specs = (
        P("seq", "ctx", None),
        P("seq", "ctx", None),
        P("seq", "ctx", None),
        P("seq", None, "ctx"),
        P("seq", None, "ctx"),
    )
    return jax.shard_map(
        per_device, mesh=mesh, in_specs=in_specs, out_specs=out_specs, check_vma=False
    )
```

time: 1050 us -> 191 us (0.18)
  waiting for transfers between devices: 702 us -> 0 us
  Pallas kernels: 0 us -> 178 us
  local copies, waits for them, and re-layouts: 145 us -> 10.9 us
  matrix products: 75.2 us -> 0 us
  blocking collectives: 59.3 us -> 0 us
  other arithmetic: 48.7 us -> 0.66 us
  between operations: 14.4 us -> 0.67 us
    reduce_scatter x4 -> x0, waiting for transfers between devices: 491 us -> none  [the longest x1 215 us: per_device(): lax.psum_scatter(adapter_terms, 'ctx', scatter_dimension=0, tiled=True)]
    all_gather x3 -> x0, waiting for transfers between devices: 210 us -> none  [the longest x1 86.6 us: per_device(): lax.all_gather(value_head_states[0], 'ctx', axis=0, tiled=True)]
    pallas_call x0 -> x3, Pallas kernels: none -> 178 us  [the longest x1 99.6 us: per_device(): pl.pallas_call(functools.partial(gather_kernel, ctx_count, seq_count, gro...]
    dot_general x32 -> x0, matrix products: 75.2 us -> none  [the longest x4 14.2 us: backward_block(): jnp.einsum('kgts,tkgd->skd', probabilities.astype(jnp.bfloat16), gradient...]
    all_gather x2 -> x0, blocking collectives: 59.3 us -> none  [the longest x1 29.8 us: per_device(): lax.all_gather(document_numbers[0], 'ctx', axis=0, tiled=True)]
    dynamic_slice x37 -> x0, local copies, waits for them, and re-layouts: 55.8 us -> none  [the longest x8 19.3 us: backward_one_block(): lax.dynamic_slice_in_dim(value_gradient_sum, row_start, backward_tenant_b...]
    dynamic_update_slice x12 -> x0, local copies, waits for them, and re-layouts: 22.6 us -> none  [the longest x8 16.4 us: backward_one_block(): lax.dynamic_update_slice_in_dim(value_gradient_sum, old_value + value_par...]
    reduce_sum x4 -> x0, other arithmetic: 13.3 us -> none  [forward_block(): weight_total = weight_total * factor + jnp.sum(weights, axis=-1)]
  transfers between devices with their start and end apart: 7 -> 0, of which waited for: 7 -> 0; matrix products, arithmetic and copies ran while one was open for 3% -> 0% of each run, Pallas kernels for 0% -> 0%
where the time goes in v1:
time: 191 us; the launch traced here: 190 us
  Pallas kernels  178 us (93%)
  local copies, waits for them, and re-layouts  10.9 us (6%)
    pallas_call x1, Pallas kernels, per_device(): pl.pallas_call(functools.partial(gather_kernel, ctx_count, seq_count, gro...  99.6 us
    pallas_call x1, Pallas kernels, per_device(): pl.pallas_call(functools.partial(reduce_kernel, ctx_count, seq_count, gro...  60 us
    pallas_call x1, Pallas kernels, per_device(): pl.pallas_call(attention_kernel, name='attention_one_head', out_shape=(sh...  18.6 us
    unnamed x20, local copies, waits for them, and re-layouts  10 us

profile of v1, /device:TPU:1, one launch (start us, length us, event | category | flops | bytes accessed | tf_op | source)
XLA Modules:
  0.0 190.3 jit_solution(18115592831731020808)
XLA Ops:
  0.6 0.0 copy-start.5
  0.6 0.7 broadcast_in_dim.20
  1.4 0.1 broadcast_in_dim.21
  1.5 0.7 pad_add_fusion
  2.1 0.8 copy.15.adapters
  2.9 0.0 copy-done.5
  2.9 0.0 copy-start
  2.9 1.2 copy-done
  4.1 0.0 copy-start.1
  4.1 1.0 copy-done.1
  5.2 0.0 copy-start.2
  5.2 1.0 copy-done.2
  6.2 0.0 copy-start.3
  6.2 0.9 copy-done.3
  7.1 0.0 copy-start.4
  7.1 0.9 copy-done.4
  8.0 0.0 copy-start.6
  8.0 0.7 copy-done.6
  8.7 99.6 %gather_heads.1 = (bf16[2048,256]{1,0:T(8,128)(2,1)S(1)}, bf16[2048,128]{1,0:T(8,128)(2,1)S(1)}, bf16[2048,128]{1,0:T(8,128)(2,1)S(1)}, bf16[2048,128]{1,0:T(8,1...) custom-call(bf16[128,4096]{1,0:T(8,128)(2,1)S(1)} %bitcast.13, ...), custom_call_target="tpu_custom_call" | custom-call | tf_op jit(solution)/shard_map/gather_heads/pallas_call | solution.py:584
  108.3 18.6 %attention_one_head.1 = (bf16[2048,128]{1,0:T(8,128)(2,1)S(1)}, bf16[2048,128]{1,0:T(8,128)(2,1)S(1)}, bf16[2048,128]{1,0:T(8,128)(2,1)S(1)}, bf16[64,2048]{1,0:T(8,128)(2,1)S(1)}, bf16[16,64,128]{2,1,0:T(8,128)(2,1)S(1)}) custom-call(bf16[2048,128]{1,0:T(8,128)(2,1)S(1)} %get-tuple-element.23.base, bf16[2048,128]{1,0:T(8,128)(2,1)S(1)} %get-tuple-element.24.key, ...), custom_call_target="tpu_custom_call" | custom-call | tf_op jit(solution)/shard_map/attention_one_head/pallas_call | solution.py:628
  126.9 60.0 %return_and_reduce.1 = (bf16[128,2048]{1,0:T(8,128)(2,1)S(1)}, f32[128,512]{1,0:T(8,128)S(1)}, f32[128,512]{1,0:T(8,128)S(1)}, f32[64,256]{1,0:T(8,128)S(1)}, f32[64,128]{1,0:T(8,128)S(1)}) custom-call(bf16[2048,128]{1,0:T(8,128)(2,1)S(1)} %get-tuple-element.30.out, bf16[2048,128]{1,0:T(8,128)(2,1)S(1)} %get-tuple-element.31.key_part, ...), custom_call_target="tpu_custom_call" | custom-call | tf_op jit(solution)/shard_map/return_and_reduce/pallas_call | solution.py:663
  186.9 0.8 copy.23
  187.7 0.7 copy.24
  188.4 0.7 copy.25
  189.1 0.6 copy.26
  189.7 0.6 copy.27
  (1 shorter events, 0.0 us)
Async XLA Ops:
  0.6 2.3 %copy-start.5 = (bf16[1,64,256]{2,1,0:T(8,128)(2,1)S(1)}, bf16[1,64,256]{2,1,0:T(8,128)(2,1)}, u32[]{:S(2)}) copy-start(bf16[1,64,256]{2,1,0:T(8,128)(2,1)} %param.17) | copy-start | bytes 98308
  2.9 1.2 copy-start
  4.1 1.0 copy-start.1
  5.2 1.0 copy-start.2
  6.2 0.9 copy-start.3
  7.1 0.9 copy-start.4
  8.0 0.7 copy-start.6

commit v2 on v0

v2 whole, which is shorter than its diff:
```python
import functools
import math

import jax
import jax.numpy as jnp
from jax import lax
from jax.experimental import pallas as pl
from jax.experimental.pallas import tpu as pltpu
from jax.sharding import PartitionSpec as P

MESH = pl.DeviceIdType.MESH
BF16 = jnp.bfloat16
F32 = jnp.float32
HEAD = 128
RANK = 64
TB = 32
KEY_BLOCK = 512
MASKED = -1e30
SCALE = 1.0 / math.sqrt(HEAD)
LOG2E = math.log2(math.e)


def dot(a, b):
    return lax.dot_general(a, b, (((1,), (0,)), ((), ())), preferred_element_type=F32)


def dot_nt(a, b):
    return lax.dot_general(a, b, (((1,), (1,)), ((), ())), preferred_element_type=F32)


def aligned(index, size):
    return pl.ds(pl.multiple_of(index * size, size), size)


def push(source, target, send, recv, dest):
    return pltpu.make_async_remote_copy(
        src_ref=source,
        dst_ref=target,
        send_sem=send,
        recv_sem=recv,
        device_id=dest,
        device_id_type=MESH,
    )


def loop(low, high, body):
    def step(index, carry):
        body(index)
        return carry

    lax.fori_loop(low, high, step, 0)


class Exchange:
    def __init__(self, axis, count, me, source, target, send, recv, local):
        self.axis, self.count, self.me = axis, count, me
        self.source, self.target = source, target
        self.send, self.recv, self.local = send, recv, local

    def copy(self, peer, place):
        return push(
            self.source(peer),
            self.target(place),
            self.send.at[peer],
            self.recv.at[place],
            {self.axis: peer},
        )

    def own(self):
        return pltpu.make_async_copy(self.source(self.me), self.target(self.me), self.local)

    def each(self, body):
        loop(1, self.count, lambda shift: body(lax.rem(self.me + shift, self.count)))

    def start(self):
        self.each(lambda peer: self.copy(peer, self.me).start())
        self.own().start()

    def wait_from(self, place):
        self.copy(place, place).wait_recv()

    def wait_recv(self):
        self.each(self.wait_from)
        self.own().wait()

    def wait_send(self):
        self.each(lambda peer: self.copy(peer, self.me).wait_send())


class Column:
    def __init__(self, planes, plane, side, send, recv):
        self.planes, self.plane, self.side = planes, plane, side
        self.send, self.recv = send, recv

    def to_plane(self, source, target, there):
        dest = {"ctx": there * 2 + self.side}
        push(source, target, self.send.at[there], self.recv.at[self.plane], dest).start()

    def to_twin(self, source, target, index):
        dest = {"ctx": self.plane * 2 + 1 - self.side}
        push(source, target, self.send.at[index], self.recv.at[index], dest).start()

    def got(self, target, index):
        dest = {"ctx": self.plane * 2 + 1 - self.side}
        push(target, target, self.send.at[index], self.recv.at[index], dest).wait_recv()

    def sent(self, source, index):
        dest = {"ctx": self.plane * 2 + 1 - self.side}
        push(source, source, self.send.at[index], self.recv.at[index], dest).wait_send()

    def others(self, body):
        loop(1, self.planes, lambda shift: body(lax.rem(self.plane + shift, self.planes)))

    def every(self, body):
        loop(0, self.planes, lambda shift: body(lax.rem(self.plane + shift, self.planes)))


def meet(me_ctx, ctx_count, me_seq, seq_count):
    barrier = pltpu.get_barrier_semaphore()

    def greet(axis, me, count):
        def step(shift):
            pl.semaphore_signal(
                barrier,
                inc=1,
                device_id={axis: lax.rem(me + shift, count)},
                device_id_type=MESH,
            )

        loop(1, count, step)

    greet("ctx", me_ctx, ctx_count)
    greet("seq", me_seq, seq_count)
    pl.semaphore_wait(barrier, ctx_count + seq_count - 2)


def spread_slots(slot_row, low, picks):
    zero = jnp.zeros_like(low)
    return jnp.concatenate(
        [jnp.where(slot_row == pick, low, zero) for pick in range(picks)], axis=0
    )


def fold_slots(slot_row, each, picks):
    total = jnp.zeros((RANK, each.shape[1]), F32)
    for pick in range(picks):
        part = each[pick * RANK : (pick + 1) * RANK]
        total = total + jnp.where(slot_row == pick, part, 0.0)
    return total


def fused_kernel(
    ctx_count,
    seq_count,
    group,
    tokens,
    base,
    key,
    value,
    gradient,
    meta,
    down,
    up,
    adapters,
    attention,
    key_grad,
    value_grad,
    down_grad,
    up_grad,
    tokens_all,
    base_all,
    key_all,
    value_all,
    gradient_all,
    meta_all,
    down_tenants,
    up_tenants,
    down_picked,
    up_picked,
    up_t,
    low_part,
    low_pair,
    low_sum,
    low_recv,
    low_all,
    grad_part,
    grad_pair,
    grad_sum,
    grad_recv,
    grad_all,
    queries_all,
    out_all,
    weights,
    scores,
    stats,
    key_t,
    value_t,
    key_sum,
    value_sum,
    key_out,
    key_pair,
    key_mid,
    key_recv,
    value_out,
    value_pair,
    value_mid,
    value_recv,
    up_sum,
    up_table,
    up_recv,
    down_sum,
    down_table,
    down_recv,
    send,
    recv,
    send_z,
    recv_z,
    send_seq,
    recv_seq,
    local,
):
    me = lax.axis_index("ctx")
    own_seq = lax.axis_index("seq")
    planes = ctx_count // 2
    plane, side = me // 2, lax.rem(me, 2)
    other = 1 - side
    rows = tokens.shape[0]
    block = 2 * rows
    length = tokens_all.shape[0]
    width = tokens_all.shape[1]
    picks = adapters.shape[1]
    key_block = min(KEY_BLOCK, length)

    def over_ctx(slot, source, target):
        return Exchange(
            "ctx", ctx_count, me, source, target, send.at[slot], recv.at[slot], local.at[slot]
        )

    def over_seq(slot, source, target):
        return Exchange(
            "seq",
            seq_count,
            own_seq,
            source,
            target,
            send_seq.at[slot],
            recv_seq.at[slot],
            local.at[5 + slot],
        )

    columns = [
        Column(planes, plane, side, send_z.at[slot], recv_z.at[slot])
        for slot in range(send_z.shape[0])
    ]
    x_move = over_ctx(
        0,
        lambda peer: tokens.at[:, aligned(peer, width)],
        lambda place: tokens_all.at[aligned(place, rows), :],
    )
    meta_move = over_ctx(
        1, lambda peer: meta, lambda place: meta_all.at[:, aligned(place, rows)]
    )
    base_move = over_ctx(
        2,
        lambda peer: base.at[:, aligned(peer, HEAD)],
        lambda place: base_all.at[aligned(place, rows), :],
    )
    gradient_move = over_ctx(
        3,
        lambda peer: gradient.at[:, aligned(peer, HEAD)],
        lambda place: gradient_all.at[aligned(place, rows), :],
    )
    out_move = over_ctx(
        4,
        lambda peer: out_all.at[aligned(peer, rows), :],
        lambda place: attention.at[:, aligned(place, HEAD)],
    )
    down_move = over_seq(0, lambda peer: down, lambda place: down_tenants.at[place])
    up_move = over_seq(1, lambda peer: up, lambda place: up_tenants.at[place])
    up_back = over_seq(2, lambda peer: up_table.at[peer], lambda place: up_recv.at[place])
    down_back = over_seq(3, lambda peer: down_table.at[peer], lambda place: down_recv.at[place])
    both = (
        (key, key_all, columns[0], columns[1], local.at[9]),
        (value, value_all, columns[2], columns[3], local.at[10]),
    )

    meet(me, ctx_count, own_seq, seq_count)
    down_move.start()
    meta_move.start()
    x_move.start()
    up_move.start()

    def head_of(there):
        return aligned((2 * there) // group, HEAD)

    def own_rows():
        return aligned(me, rows)

    for source, target, column, _, own_sem in both:
        column.others(
            lambda there, source=source, target=target, column=column: column.to_plane(
                source.at[:, head_of(there)], target.at[own_rows(), :], there
            )
        )
        pltpu.make_async_copy(
            source.at[:, head_of(plane)], target.at[own_rows(), :], own_sem
        ).start()
    base_move.start()

    meta_move.wait_recv()
    down_move.wait_recv()
    for pick in range(picks):
        down_picked[pick * RANK : (pick + 1) * RANK, :] = down_tenants[adapters[own_seq, pick]]

    low_pair_column, low_column, low_gather, low_share = columns[4:8]
    x_move.own().wait()

    def low_step(there):
        for part in range(2):
            place = 2 * there + part

            @pl.when(place != me)
            def _():
                x_move.wait_from(place)

        cols = aligned(there, block)
        each = dot_nt(down_picked[...], tokens_all[cols, :])
        low = fold_slots(meta_all[1:2, cols], each, picks).astype(BF16)
        low_part[there, 0] = low[:, :rows]
        low_part[there, 1] = low[:, rows:]
        low_pair_column.to_twin(low_part.at[there, other], low_pair.at[there], there)

    columns[4].every(low_step)

    def reduce_column(pair_column, column, part, pair, total, recv_ref):
        def pair_step(there):
            pair_column.got(pair.at[there], there)
            total[there] = (
                part[there, side].astype(F32) + pair[there].astype(F32)
            ).astype(BF16)

            @pl.when(there != plane)
            def _():
                column.to_plane(total.at[there], recv_ref.at[plane], there)

        column.every(pair_step)

    def finish_column(column, total, recv_ref):
        recv_ref[plane] = total[plane]
        column.others(lambda there: column.got(recv_ref.at[there], there))
        return lax.fori_loop(
            0,
            planes,
            lambda there, acc: acc + recv_ref[there].astype(F32),
            jnp.zeros((RANK, rows), F32),
        ).astype(BF16)

    def gather_start(column, share, all_ref):
        column.others(lambda there: column.to_plane(all_ref.at[me], all_ref.at[me], there))
        share.to_twin(all_ref.at[me], all_ref.at[me], plane)

    def gather_finish(column, share, all_ref):
        def forward(there):
            place = 2 * there + side
            column.got(all_ref.at[place], there)
            share.to_twin(all_ref.at[place], all_ref.at[place], there)

        column.others(forward)
        share.every(lambda there: share.got(all_ref.at[2 * there + other], there))

    reduce_column(low_pair_column, low_column, low_part, low_pair, low_sum, low_recv)
    gradient_move.start()
    low_all[me] = finish_column(low_column, low_sum, low_recv)
    gather_start(low_gather, low_share, low_all)

    for source, target, column, share, own_sem in both:
        pltpu.make_async_copy(
            source.at[:, head_of(plane)], target.at[own_rows(), :], own_sem
        ).wait()

        def forward(there, target=target, column=column, share=share):
            place = target.at[aligned(2 * there + side, rows), :]

            @pl.when(there != plane)
            def _():
                column.got(place, there)

            share.to_twin(place, place, there)

        column.every(forward)
    gather_finish(low_gather, low_share, low_all)
    up_move.wait_recv()
    for pick in range(picks):
        up_picked[pick * RANK : (pick + 1) * RANK, :] = up_tenants[adapters[own_seq, pick]]
    up_t[...] = jnp.transpose(up_picked[...])
    for source, target, column, share, own_sem in both:
        share.every(
            lambda there, target=target, share=share: share.got(
                target.at[aligned(2 * there + other, rows), :], there
            )
        )
    key_t[...] = jnp.transpose(key_all[...])
    value_t[...] = jnp.transpose(value_all[...])
    base_move.wait_recv()

    documents = meta_all[0:1, :]
    cuts = [
        jnp.sum(jnp.where(documents < number, 1, 0), axis=1, keepdims=True) for number in (1, 2, 3)
    ]

    def slots_of(there, all_ref):
        slot_row = meta_all[1:2, aligned(there, block)]
        low = jnp.concatenate([all_ref[2 * there], all_ref[2 * there + 1]], axis=1)
        return slot_row, spread_slots(slot_row, low, picks)

    def blocks_of(there):
        return (there * block + block - 1) // key_block + 1

    def forward_step(there):
        place = aligned(there, block)
        _, low_spread = slots_of(there, low_all)
        lifted = dot(up_t[...], low_spread)
        queries = (base_all[place, :].astype(F32) + jnp.transpose(lifted)).astype(BF16)
        queries_all[place, :] = queries
        position = there * block + lax.broadcasted_iota(jnp.int32, (1, block), 1)
        start = jnp.zeros((1, block), jnp.int32)
        for cut in cuts:
            start = jnp.where(position >= cut, cut, start)

        def score_step(index, peak):
            keys = aligned(index, key_block)
            logits = dot_nt(key_all[keys, :], queries) * (SCALE * LOG2E)
            key_position = index * key_block + lax.broadcasted_iota(
                jnp.int32, (key_block, block), 0
            )
            logits = jnp.where(
                (key_position <= position) & (key_position >= start), logits, MASKED
            )
            scores[keys, :] = logits
            return jnp.maximum(peak, jnp.max(logits.reshape(-1, 8, block), axis=0))

        peak8 = lax.fori_loop(
            0, blocks_of(there), score_step, jnp.full((8, block), MASKED, F32)
        )
        peak = jnp.max(peak8, axis=0, keepdims=True)

        def weight_step(index, state):
            total, mixed = state
            keys = aligned(index, key_block)
            weight = jnp.exp2(scores[keys, :] - peak)
            weight_low = weight.astype(BF16)
            weights[there, keys, :] = weight_low
            total = total + jnp.sum(weight.reshape(-1, 8, block), axis=0)
            return total, mixed + dot(value_t[:, keys], weight_low)

        total8, mixed = lax.fori_loop(
            0,
            blocks_of(there),
            weight_step,
            (jnp.zeros((8, block), F32), jnp.zeros((HEAD, block), F32)),
        )
        inverse = 1.0 / jnp.sum(total8, axis=0, keepdims=True)
        stats[there] = jnp.broadcast_to(inverse, (8, block))
        out_all[place, :] = jnp.transpose((mixed * inverse).astype(BF16))
        for part in range(2):
            dest = 2 * there + part

            @pl.when(dest != me)
            def _():
                out_move.copy(dest, me).start()

    columns[0].every(forward_step)
    out_move.own().start()
    gradient_move.wait_recv()
    key_sum[...] = jnp.zeros_like(key_sum)
    value_sum[...] = jnp.zeros_like(value_sum)
    up_sum[...] = jnp.zeros_like(up_sum)

    key_x, value_x, grad_x, key_z, value_z, grad_z, grad_gather, grad_share = columns[8:16]

    def backward_step(step):
        there = planes - 1 - step
        place = aligned(there, block)
        slot_row, low_spread = slots_of(there, low_all)
        queries = queries_all[place, :]
        gradient_t = jnp.transpose(gradient_all[place, :]).astype(F32) * stats[there, 0:1, :]
        out_t = jnp.transpose(out_all[place, :]).astype(F32)
        delta = jnp.sum(gradient_t * out_t, axis=0, keepdims=True)
        gradient_low = jnp.transpose(gradient_t.astype(BF16))

        def back_step(index, query_sum):
            keys = aligned(index, key_block)
            weight_low = weights[there, keys, :]
            value_sum[keys, :] += dot(weight_low, gradient_low)
            dprobs = dot_nt(value_all[keys, :], gradient_low)
            dscores = (weight_low.astype(F32) * (dprobs - delta)).astype(BF16)
            key_sum[keys, :] += dot(dscores, queries)
            return query_sum + dot(key_t[:, keys], dscores)

        query_sum = lax.fori_loop(
            0, blocks_of(there), back_step, jnp.zeros((HEAD, block), F32)
        )
        query_grad = (query_sum * SCALE).astype(BF16)
        each = dot(up_picked[...], query_grad)
        low = fold_slots(slot_row, each, picks).astype(BF16)
        grad_part[there, 0] = low[:, :rows]
        grad_part[there, 1] = low[:, rows:]
        up_sum[...] += dot_nt(low_spread, query_grad)
        for part in range(2):
            half = aligned(2 * there + part, rows)
            key_out[there, part] = (key_sum[half, :] * SCALE).astype(BF16)
            value_out[there, part] = value_sum[half, :].astype(BF16)
        grad_x.to_twin(grad_part.at[there, other], grad_pair.at[there], there)
        key_x.to_twin(key_out.at[there, other], key_pair.at[there], there)
        value_x.to_twin(value_out.at[there, other], value_pair.at[there], there)

        @pl.when(step > 0)
        def _():
            pass_on(there + 1)

    def pass_on(there):
        for pair_column, column, part, pair, total, recv_ref in (
            (grad_x, grad_z, grad_part, grad_pair, grad_sum, grad_recv),
            (key_x, key_z, key_out, key_pair, key_mid, key_recv),
            (value_x, value_z, value_out, value_pair, value_mid, value_recv),
        ):
            pair_column.got(pair.at[there], there)
            total[there] = (
                part[there, side].astype(F32) + pair[there].astype(F32)
            ).astype(BF16)

            @pl.when(there != plane)
            def _():
                column.to_plane(total.at[there], recv_ref.at[plane], there)

    loop(0, planes, backward_step)
    pass_on(0)

    tenants = [adapters[own_seq, pick] for pick in range(picks)]

    def build_table(total_ref, table_ref):
        def table_step(tenant):
            total = jnp.zeros((RANK, total_ref.shape[1]), F32)
            for pick in range(picks):
                here = (tenants[pick] == tenant).astype(F32)
                total = total + total_ref[pick * RANK : (pick + 1) * RANK, :] * here
            table_ref[tenant] = total.astype(BF16)

        loop(0, seq_count, table_step)

    build_table(up_sum, up_table)
    up_back.start()
    grad_all[me] = finish_column(grad_z, grad_sum, grad_recv)
    gather_start(grad_gather, grad_share, grad_all)
    gather_finish(grad_gather, grad_share, grad_all)
    down_sum[...] = jnp.zeros_like(down_sum)

    def down_step(there):
        _, spread = slots_of(there, grad_all)
        down_sum[...] += dot(spread, tokens_all[aligned(there, block), :])

    loop(0, planes, down_step)
    build_table(down_sum, down_table)
    down_back.start()

    members = group // 2
    for column, total, recv_ref, grad in (
        (key_z, key_mid, key_recv, key_grad),
        (value_z, value_mid, value_recv, value_grad),
    ):
        recv_ref[plane] = total[plane]
        column.others(
            lambda there, column=column, recv_ref=recv_ref: column.got(recv_ref.at[there], there)
        )
        for head in range(planes // members):
            acc = recv_ref[head * members].astype(F32)
            for member in range(1, members):
                acc = acc + recv_ref[head * members + member].astype(F32)
            grad[:, head * HEAD : (head + 1) * HEAD] = acc

    def add_up(recv_ref, grad):
        grad[...] = lax.fori_loop(
            0,
            seq_count,
            lambda index, acc: acc + recv_ref[index].astype(F32),
            jnp.zeros(grad.shape, F32),
        )

    up_back.wait_recv()
    add_up(up_recv, up_grad)
    out_move.wait_recv()
    down_back.wait_recv()
    add_up(down_recv, down_grad)

    for move in (
        x_move,
        meta_move,
        base_move,
        gradient_move,
        out_move,
        down_move,
        up_move,
        up_back,
        down_back,
    ):
        move.wait_send()
    for source, target, column, share, _ in both:
        column.others(
            lambda there, source=source, column=column: column.sent(
                source.at[:, head_of(there)], there
            )
        )
        share.every(
            lambda there, target=target, share=share: share.sent(
                target.at[aligned(2 * there + side, rows), :], there
            )
        )
    for pair_column, part in (
        (low_pair_column, low_part),
        (grad_x, grad_part),
        (key_x, key_out),
        (value_x, value_out),
    ):
        pair_column.every(
            lambda there, pair_column=pair_column, part=part: pair_column.sent(
                part.at[there, other], there
            )
        )
    for column, total in (
        (low_column, low_sum),
        (grad_z, grad_sum),
        (key_z, key_mid),
        (value_z, value_mid),
    ):
        column.others(
            lambda there, column=column, total=total: column.sent(total.at[there], there)
        )
    for column, share, all_ref in (
        (low_gather, low_share, low_all),
        (grad_gather, grad_share, grad_all),
    ):
        column.others(lambda there, column=column, all_ref=all_ref: column.sent(all_ref.at[me], there))
        share.every(
            lambda there, share=share, all_ref=all_ref: share.sent(
                all_ref.at[2 * there + side], there
            )
        )


def vmem():
    return pl.BlockSpec(memory_space=pltpu.VMEM)


def hbm():
    return pl.BlockSpec(memory_space=pltpu.HBM)


def smem():
    return pl.BlockSpec(memory_space=pltpu.SMEM)


def per_device(
    normed_hidden_input,
    frozen_query_base,
    key_head_states,
    value_head_states,
    document_numbers,
    tenant_block_entry,
    sequence_adapter_list,
    adapter_down_weight,
    adapter_up_weight,
    output_gradient,
):
    ctx_count = lax.axis_size("ctx")
    seq_count = lax.axis_size("seq")
    planes = ctx_count // 2
    rows = normed_hidden_input.shape[1]
    length = rows * ctx_count
    width = adapter_down_weight.shape[2]
    picks = sequence_adapter_list.shape[1]
    key_heads = key_head_states.shape[2] // HEAD
    group = ctx_count // key_heads
    stacked = picks * RANK
    token_slots = jnp.repeat(tenant_block_entry, TB, axis=1)
    meta = jnp.pad(jnp.concatenate([document_numbers, token_slots], axis=0), ((0, 6), (0, 0)))

    def shape(dims, dtype=BF16):
        return jax.ShapeDtypeStruct(dims, dtype)

    head_rows = pltpu.VMEM((length, HEAD), BF16)
    low_plane = pltpu.VMEM((planes, RANK, rows), BF16)
    low_halves = pltpu.VMEM((planes, 2, RANK, rows), BF16)
    low_blocks = pltpu.VMEM((ctx_count, RANK, rows), BF16)
    low_buffers = [low_halves, low_plane, low_plane, low_plane, low_blocks]
    key_plane = pltpu.VMEM((planes, rows, HEAD), BF16)
    key_buffers = [pltpu.VMEM((planes, 2, rows, HEAD), BF16), key_plane, key_plane, key_plane]
    attention, key_grad, value_grad, down_grad, up_grad = pl.pallas_call(
        functools.partial(fused_kernel, ctx_count, seq_count, group),
        name="attention_layer",
        out_shape=(
            shape((rows, ctx_count * HEAD)),
            shape((rows, key_heads * HEAD), F32),
            shape((rows, key_heads * HEAD), F32),
            shape((RANK, width), F32),
            shape((RANK, HEAD), F32),
        ),
        in_specs=[hbm()] * 8 + [smem()],
        out_specs=(hbm(), vmem(), vmem(), vmem(), vmem()),
        scratch_shapes=[
            pltpu.VMEM((length, width), BF16),
            head_rows,
            head_rows,
            head_rows,
            head_rows,
            pltpu.VMEM((8, length), jnp.int32),
            pltpu.VMEM((seq_count, RANK, width), BF16),
            pltpu.VMEM((seq_count, RANK, HEAD), BF16),
            pltpu.VMEM((stacked, width), BF16),
            pltpu.VMEM((stacked, HEAD), BF16),
            pltpu.VMEM((HEAD, stacked), BF16),
            *low_buffers,
            *low_buffers,
            head_rows,
            head_rows,
            pltpu.VMEM((planes, length, 2 * rows), BF16),
            pltpu.VMEM((length, 2 * rows), F32),
            pltpu.VMEM((planes, 8, 2 * rows), F32),
            pltpu.VMEM((HEAD, length), BF16),
            pltpu.VMEM((HEAD, length), BF16),
            pltpu.VMEM((length, HEAD), F32),
            pltpu.VMEM((length, HEAD), F32),
            *key_buffers,
            *key_buffers,
            pltpu.VMEM((stacked, HEAD), F32),
            pltpu.VMEM((seq_count, RANK, HEAD), BF16),
            pltpu.VMEM((seq_count, RANK, HEAD), BF16),
            pltpu.VMEM((stacked, width), F32),
            pltpu.VMEM((seq_count, RANK, width), BF16),
            pltpu.VMEM((seq_count, RANK, width), BF16),
            pltpu.SemaphoreType.DMA((5, ctx_count)),
            pltpu.SemaphoreType.DMA((5, ctx_count)),
            pltpu.SemaphoreType.DMA((16, planes)),
            pltpu.SemaphoreType.DMA((16, planes)),
            pltpu.SemaphoreType.DMA((4, seq_count)),
            pltpu.SemaphoreType.DMA((4, seq_count)),
            pltpu.SemaphoreType.DMA((11,)),
        ],
        compiler_params=pltpu.CompilerParams(
            collective_id=0, has_side_effects=True, vmem_limit_bytes=56 << 20
        ),
    )(
        normed_hidden_input[0],
        frozen_query_base[0],
        key_head_states[0],
        value_head_states[0],
        output_gradient[0],
        meta,
        adapter_down_weight[0],
        adapter_up_weight[0],
        sequence_adapter_list,
    )
    return (
        attention[None],
        key_grad[None],
        value_grad[None],
        down_grad[None],
        up_grad[None],
    )


def solution(mesh):
    in_specs = (
        P("seq", "ctx", None),
        P("seq", "ctx", None),
        P("seq", "ctx", None),
        P("seq", "ctx", None),
        P("seq", "ctx"),
        P("seq", "ctx"),
        P(),
        P("seq", None, "ctx"),
        P("seq", None, "ctx"),
        P("seq", "ctx", None),
    )
    out_specs = (
        P("seq", "ctx", None),
        P("seq", "ctx", None),
        P("seq", "ctx", None),
        P("seq", None, "ctx"),
        P("seq", None, "ctx"),
    )
    return jax.shard_map(
        per_device, mesh=mesh, in_specs=in_specs, out_specs=out_specs, check_vma=False
    )
```

time: 1050 us -> 165 us (0.16)
  waiting for transfers between devices: 702 us -> 0 us
  Pallas kernels: 0 us -> 156 us
  local copies, waits for them, and re-layouts: 145 us -> 7.93 us
  matrix products: 75.2 us -> 0 us
  blocking collectives: 59.3 us -> 0 us
  other arithmetic: 48.7 us -> 0.01 us
  between operations: 14.4 us -> 0.67 us
    reduce_scatter x4 -> x0, waiting for transfers between devices: 491 us -> none  [the longest x1 215 us: per_device(): lax.psum_scatter(adapter_terms, 'ctx', scatter_dimension=0, tiled=True)]
    all_gather x3 -> x0, waiting for transfers between devices: 210 us -> none  [the longest x1 86.6 us: per_device(): lax.all_gather(value_head_states[0], 'ctx', axis=0, tiled=True)]
    pallas_call x0 -> x1, Pallas kernels: none -> 156 us  [per_device(): pl.pallas_call(functools.partial(fused_kernel, ctx_count, seq_count, grou...]
    dot_general x32 -> x0, matrix products: 75.2 us -> none  [the longest x4 14.2 us: backward_block(): jnp.einsum('kgts,tkgd->skd', probabilities.astype(jnp.bfloat16), gradient...]
    all_gather x2 -> x0, blocking collectives: 59.3 us -> none  [the longest x1 29.8 us: per_device(): lax.all_gather(document_numbers[0], 'ctx', axis=0, tiled=True)]
    dynamic_slice x37 -> x0, local copies, waits for them, and re-layouts: 55.8 us -> none  [the longest x8 19.3 us: backward_one_block(): lax.dynamic_slice_in_dim(value_gradient_sum, row_start, backward_tenant_b...]
    dynamic_update_slice x12 -> x0, local copies, waits for them, and re-layouts: 22.6 us -> none  [the longest x8 16.4 us: backward_one_block(): lax.dynamic_update_slice_in_dim(value_gradient_sum, old_value + value_par...]
    reduce_sum x4 -> x0, other arithmetic: 13.3 us -> none  [forward_block(): weight_total = weight_total * factor + jnp.sum(weights, axis=-1)]
  transfers between devices with their start and end apart: 7 -> 0, of which waited for: 7 -> 0; matrix products, arithmetic and copies ran while one was open for 3% -> 0% of each run, Pallas kernels for 0% -> 0%
where the time goes in v2:
time: 165 us; the launch traced here: 164 us
  Pallas kernels  156 us (95%)
  local copies, waits for them, and re-layouts  7.93 us (5%)
    pallas_call x1, Pallas kernels, per_device(): pl.pallas_call(functools.partial(fused_kernel, ctx_count, seq_count, grou...  156 us
    unnamed x20, local copies, waits for them, and re-layouts  7.18 us

profile of v2, /device:TPU:1, one launch (start us, length us, event | category | flops | bytes accessed | tf_op | source)
XLA Modules:
  0.0 164.4 jit_solution(17205365011638622797)
XLA Ops:
  0.6 0.0 copy-start.5
  0.6 0.6 copy-done.5
  1.3 0.1 broadcast_in_dim.20
  1.4 0.0 copy-start.6
  1.4 0.1 broadcast_in_dim.21
  1.4 0.6 copy-done.6
  2.0 0.0 copy-start.4
  2.0 0.6 pad.4.meta
  2.6 0.1 copy-done.4
  2.7 0.7 copy.15.adapters
  3.4 155.8 %attention_layer.1 = (bf16[128,2048]{1,0:T(8,128)(2,1)}, f32[128,512]{1,0:T(8,128)}, f32[128,512]{1,0:T(8,128)}, f32[64,256]{1,0:T(8,128)}, f32[64,128]{1,0:T(8,128)}) custom-call(bf16[128,4096]{1,0:T(8,128)(2,1)} %bitcast.13, bf16[128,2048]{1,0:T(8,128)(2,1)} %bitcast.14, bf16[128,512]{1,0:T(8,128)(2,1)} %bitcast.19, bf16[128,512]{1,0:T(8,128)(2,1)} %bitcast.20, ...), custom_call_target="tpu_custom_call" | custom-call | tf_op jit(solution)/shard_map/attention_layer/pallas_call | solution.py:697
  159.2 0.0 copy-start.1
  159.2 1.9 %copy.21 = bf16[1,128,2048]{2,1,0:T(8,128)(2,1)} copy(bf16[1,128,2048]{2,1,0:T(8,128)(2,1)} %bitcast.16) | data formatting | bytes 1048576
  161.1 0.0 copy-done.1
  161.1 0.0 copy-start
  161.1 0.7 copy.22
  161.8 0.3 copy-done
  162.1 0.0 copy-start.2
  162.1 0.7 copy.23
  162.9 0.2 copy-done.2
  163.0 0.0 copy-start.3
  163.0 0.6 copy.24
  163.6 0.1 copy-done.3
  163.8 0.6 copy.25
  (1 shorter events, 0.0 us)
Async XLA Ops:
  0.6 0.7 copy-start.5
  1.4 0.7 copy-start.6
  2.0 0.7 copy-start.4
  159.2 1.9 %copy-start.1 = (f32[128,512]{1,0:T(8,128)S(1)}, f32[128,512]{1,0:T(8,128)}, u32[]{:S(2)}) copy-start(f32[128,512]{1,0:T(8,128)} %get-tuple-element.11) | copy-start | bytes 786436
  161.1 1.0 copy-start
  162.1 0.9 copy-start.2
  163.0 0.8 copy-start.3

commit v3 on v2

--- a/solution.py
+++ b/solution.py
@@ -74,14 +74,20 @@
 
     def start(self):
         self.each(lambda peer: self.copy(peer, self.me).start())
-        self.own().start()
+        if self.local is not None:
+            self.own().start()
 
     def wait_from(self, place):
         self.copy(place, place).wait_recv()
 
     def wait_recv(self):
-        self.each(self.wait_from)
-        self.own().wait()
+        loop(
+            1,
+            self.count,
+            lambda shift: self.wait_from(lax.rem(self.me + self.count - shift, self.count)),
+        )
+        if self.local is not None:
+            self.own().wait()
 
     def wait_send(self):
         self.each(lambda peer: self.copy(peer, self.me).wait_send())
@@ -113,6 +119,18 @@
 
     def every(self, body):
         loop(0, self.planes, lambda shift: body(lax.rem(self.plane + shift, self.planes)))
+
+    def away(self, step):
+        left = self.planes - step
+        shift = jnp.where(lax.rem(left, 2) == 0, left // 2, -(left // 2))
+        return lax.rem(self.plane + self.planes + shift, self.planes)
+
+    def arrivals(self, body, first=0):
+        loop(
+            first,
+            self.planes,
+            lambda shift: body(lax.rem(self.plane + self.planes - shift, self.planes)),
+        )
 
 
 def meet(me_ctx, ctx_count, me_seq, seq_count):
@@ -179,24 +197,19 @@
     up_picked,
     up_t,
     low_part,
-    low_pair,
-    low_sum,
     low_recv,
     low_all,
     grad_part,
-    grad_pair,
-    grad_sum,
     grad_recv,
     grad_all,
     queries_all,
     out_all,
     weights,
+    dscores_all,
     scores,
     stats,
     key_t,
     value_t,
-    key_sum,
-    value_sum,
     key_out,
     key_pair,
     key_mid,
@@ -231,9 +244,16 @@
     picks = adapters.shape[1]
     key_block = min(KEY_BLOCK, length)
 
-    def over_ctx(slot, source, target):
+    def over_ctx(slot, source, target, has_own=True):
         return Exchange(
-            "ctx", ctx_count, me, source, target, send.at[slot], recv.at[slot], local.at[slot]
+            "ctx",
+            ctx_count,
+            me,
+            source,
+            target,
+            send.at[slot],
+            recv.at[slot],
+            local.at[slot] if has_own else None,
         )
 
     def over_seq(slot, source, target):
@@ -275,6 +295,18 @@
         lambda peer: out_all.at[aligned(peer, rows), :],
         lambda place: attention.at[:, aligned(place, HEAD)],
     )
+    grad_move = over_ctx(
+        5, lambda peer: grad_part.at[peer], lambda place: grad_recv.at[place], has_own=False
+    )
+    grad_gather = over_ctx(
+        6, lambda peer: grad_all.at[me], lambda place: grad_all.at[place], has_own=False
+    )
+    low_move = over_ctx(
+        7, lambda peer: low_part.at[peer], lambda place: low_recv.at[place], has_own=False
+    )
+    low_gather = over_ctx(
+        8, lambda peer: low_all.at[me], lambda place: low_all.at[place], has_own=False
+    )
     down_move = over_seq(0, lambda peer: down, lambda place: down_tenants.at[place])
     up_move = over_seq(1, lambda peer: up, lambda place: up_tenants.at[place])
     up_back = over_seq(2, lambda peer: up_table.at[peer], lambda place: up_recv.at[place])
@@ -285,26 +317,45 @@
     )
 
     meet(me, ctx_count, own_seq, seq_count)
+
+    def head_of(there):
+        return aligned((2 * there) // group, HEAD)
+
+    def own_rows():
+        return aligned(me, rows)
+
+    def key_send():
+        for source, target, column, _, own_sem in both:
+            column.others(
+                lambda there, source=source, target=target, column=column: column.to_plane(
+                    source.at[:, head_of(there)], target.at[own_rows(), :], there
+                )
+            )
+            pltpu.make_async_copy(
+                source.at[:, head_of(plane)], target.at[own_rows(), :], own_sem
+            ).start()
+
+    def key_forward():
+        for source, target, column, share, own_sem in both:
+            pltpu.make_async_copy(
+                source.at[:, head_of(plane)], target.at[own_rows(), :], own_sem
+            ).wait()
+
+            def forward(there, target=target, column=column, share=share):
+                place = target.at[aligned(2 * there + side, rows), :]
+
+                @pl.when(there != plane)
+                def _():
+                    column.got(place, there)
+
+                share.to_twin(place, place, there)
+
+            column.arrivals(forward)
+
     down_move.start()
     meta_move.start()
     x_move.start()
     up_move.start()
-
-    def head_of(there):
-        return aligned((2 * there) // group, HEAD)
-
-    def own_rows():
-        return aligned(me, rows)
-
-    for source, target, column, _, own_sem in both:
-        column.others(
-            lambda there, source=source, target=target, column=column: column.to_plane(
-                source.at[:, head_of(there)], target.at[own_rows(), :], there
-            )
-        )
-        pltpu.make_async_copy(
-            source.at[:, head_of(plane)], target.at[own_rows(), :], own_sem
-        ).start()
     base_move.start()
 
     meta_move.wait_recv()
@@ -312,8 +363,27 @@
     for pick in range(picks):
         down_picked[pick * RANK : (pick + 1) * RANK, :] = down_tenants[adapters[own_seq, pick]]
 
-    low_pair_column, low_column, low_gather, low_share = columns[4:8]
     x_move.own().wait()
+
+    def deal(low, there, part_ref, move):
+        for part in range(2):
+            dest = 2 * there + part
+            part_ref[dest] = low[:, part * rows : (part + 1) * rows]
+
+            @pl.when(dest != me)
+            def _():
+                move.copy(dest, me).start()
+
+    def collect(part_ref, recv_ref, all_ref, move, gather):
+        recv_ref[me] = part_ref[me]
+        move.wait_recv()
+        all_ref[me] = lax.fori_loop(
+            0,
+            ctx_count,
+            lambda place, acc: acc + recv_ref[place].astype(F32),
+            jnp.zeros((RANK, rows), F32),
+        ).astype(BF16)
+        gather.start()
 
     def low_step(there):
         for part in range(2):
@@ -326,69 +396,14 @@
         cols = aligned(there, block)
         each = dot_nt(down_picked[...], tokens_all[cols, :])
         low = fold_slots(meta_all[1:2, cols], each, picks).astype(BF16)
-        low_part[there, 0] = low[:, :rows]
-        low_part[there, 1] = low[:, rows:]
-        low_pair_column.to_twin(low_part.at[there, other], low_pair.at[there], there)
-
-    columns[4].every(low_step)
-
-    def reduce_column(pair_column, column, part, pair, total, recv_ref):
-        def pair_step(there):
-            pair_column.got(pair.at[there], there)
-            total[there] = (
-                part[there, side].astype(F32) + pair[there].astype(F32)
-            ).astype(BF16)
-
-            @pl.when(there != plane)
-            def _():
-                column.to_plane(total.at[there], recv_ref.at[plane], there)
-
-        column.every(pair_step)
-
-    def finish_column(column, total, recv_ref):
-        recv_ref[plane] = total[plane]
-        column.others(lambda there: column.got(recv_ref.at[there], there))
-        return lax.fori_loop(
-            0,
-            planes,
-            lambda there, acc: acc + recv_ref[there].astype(F32),
-            jnp.zeros((RANK, rows), F32),
-        ).astype(BF16)
-
-    def gather_start(column, share, all_ref):
-        column.others(lambda there: column.to_plane(all_ref.at[me], all_ref.at[me], there))
-        share.to_twin(all_ref.at[me], all_ref.at[me], plane)
-
-    def gather_finish(column, share, all_ref):
-        def forward(there):
-            place = 2 * there + side
-            column.got(all_ref.at[place], there)
-            share.to_twin(all_ref.at[place], all_ref.at[place], there)
-
-        column.others(forward)
-        share.every(lambda there: share.got(all_ref.at[2 * there + other], there))
-
-    reduce_column(low_pair_column, low_column, low_part, low_pair, low_sum, low_recv)
-    gradient_move.start()
-    low_all[me] = finish_column(low_column, low_sum, low_recv)
-    gather_start(low_gather, low_share, low_all)
-
-    for source, target, column, share, own_sem in both:
-        pltpu.make_async_copy(
-            source.at[:, head_of(plane)], target.at[own_rows(), :], own_sem
-        ).wait()
-
-        def forward(there, target=target, column=column, share=share):
-            place = target.at[aligned(2 * there + side, rows), :]
-
-            @pl.when(there != plane)
-            def _():
-                column.got(place, there)
-
-            share.to_twin(place, place, there)
-
-        column.every(forward)
-    gather_finish(low_gather, low_share, low_all)
+        deal(low, there, low_part, low_move)
+
+    columns[0].arrivals(low_step)
+    key_send()
+
+    collect(low_part, low_recv, low_all, low_move, low_gather)
+    key_forward()
+    low_gather.wait_recv()
     up_move.wait_recv()
     for pick in range(picks):
         up_picked[pick * RANK : (pick + 1) * RANK, :] = up_tenants[adapters[own_seq, pick]]
@@ -469,32 +484,26 @@
             def _():
                 out_move.copy(dest, me).start()
 
-    columns[0].every(forward_step)
+    gradient_move.start()
+    loop(0, planes, lambda step: forward_step(columns[0].away(step)))
     out_move.own().start()
     gradient_move.wait_recv()
-    key_sum[...] = jnp.zeros_like(key_sum)
-    value_sum[...] = jnp.zeros_like(value_sum)
     up_sum[...] = jnp.zeros_like(up_sum)
 
-    key_x, value_x, grad_x, key_z, value_z, grad_z, grad_gather, grad_share = columns[8:16]
-
-    def backward_step(step):
-        there = planes - 1 - step
+    def backward_step(there):
         place = aligned(there, block)
         slot_row, low_spread = slots_of(there, low_all)
-        queries = queries_all[place, :]
         gradient_t = jnp.transpose(gradient_all[place, :]).astype(F32) * stats[there, 0:1, :]
         out_t = jnp.transpose(out_all[place, :]).astype(F32)
         delta = jnp.sum(gradient_t * out_t, axis=0, keepdims=True)
         gradient_low = jnp.transpose(gradient_t.astype(BF16))
+        gradient_all[place, :] = gradient_low
 
         def back_step(index, query_sum):
             keys = aligned(index, key_block)
-            weight_low = weights[there, keys, :]
-            value_sum[keys, :] += dot(weight_low, gradient_low)
             dprobs = dot_nt(value_all[keys, :], gradient_low)
-            dscores = (weight_low.astype(F32) * (dprobs - delta)).astype(BF16)
-            key_sum[keys, :] += dot(dscores, queries)
+            dscores = (weights[there, keys, :].astype(F32) * (dprobs - delta)).astype(BF16)
+            dscores_all[there, keys, :] = dscores
             return query_sum + dot(key_t[:, keys], dscores)
 
         query_sum = lax.fori_loop(
@@ -503,24 +512,55 @@
         query_grad = (query_sum * SCALE).astype(BF16)
         each = dot(up_picked[...], query_grad)
         low = fold_slots(slot_row, each, picks).astype(BF16)
-        grad_part[there, 0] = low[:, :rows]
-        grad_part[there, 1] = low[:, rows:]
+        deal(low, there, grad_part, grad_move)
         up_sum[...] += dot_nt(low_spread, query_grad)
+
+    loop(0, planes, lambda step: backward_step(columns[0].away(step)))
+
+    tenants = [adapters[own_seq, pick] for pick in range(picks)]
+
+    def build_table(total_ref, table_ref):
+        def table_step(tenant):
+            total = jnp.zeros((RANK, total_ref.shape[1]), F32)
+            for pick in range(picks):
+                here = (tenants[pick] == tenant).astype(F32)
+                total = total + total_ref[pick * RANK : (pick + 1) * RANK, :] * here
+            table_ref[tenant] = total.astype(BF16)
+
+        loop(0, seq_count, table_step)
+
+    build_table(up_sum, up_table)
+    up_back.start()
+
+    key_x, value_x, key_z, value_z = columns[4:8]
+
+    def key_step(shift):
+        there = key_x.away(shift)
+        place = aligned(there, block)
+
+        def query_step(index, state):
+            keys_acc, values_acc = state
+            from_rows = aligned(index, block)
+            values_acc = values_acc + dot(weights[index, place, :], gradient_all[from_rows, :])
+            keys_acc = keys_acc + dot(dscores_all[index, place, :], queries_all[from_rows, :])
+            return keys_acc, values_acc
+
+        zero = jnp.zeros((block, HEAD), F32)
+        keys_acc, values_acc = lax.fori_loop(there, planes, query_step, (zero, zero))
+        keys_low = (keys_acc * SCALE).astype(BF16)
+        values_low = values_acc.astype(BF16)
         for part in range(2):
-            half = aligned(2 * there + part, rows)
-            key_out[there, part] = (key_sum[half, :] * SCALE).astype(BF16)
-            value_out[there, part] = value_sum[half, :].astype(BF16)
-        grad_x.to_twin(grad_part.at[there, other], grad_pair.at[there], there)
+            key_out[there, part] = keys_low[part * rows : (part + 1) * rows]
+            value_out[there, part] = values_low[part * rows : (part + 1) * rows]
         key_x.to_twin(key_out.at[there, other], key_pair.at[there], there)
         value_x.to_twin(value_out.at[there, other], value_pair.at[there], there)
 
-        @pl.when(step > 0)
+        @pl.when(shift > 0)
         def _():
-            pass_on(there + 1)
+            pass_on(key_x.away(shift - 1))
 
     def pass_on(there):
         for pair_column, column, part, pair, total, recv_ref in (
-            (grad_x, grad_z, grad_part, grad_pair, grad_sum, grad_recv),
             (key_x, key_z, key_out, key_pair, key_mid, key_recv),
             (value_x, value_z, value_out, value_pair, value_mid, value_recv),
         ):
@@ -533,26 +573,11 @@
             def _():
                 column.to_plane(total.at[there], recv_ref.at[plane], there)
 
-    loop(0, planes, backward_step)
-    pass_on(0)
-
-    tenants = [adapters[own_seq, pick] for pick in range(picks)]
-
-    def build_table(total_ref, table_ref):
-        def table_step(tenant):
-            total = jnp.zeros((RANK, total_ref.shape[1]), F32)
-            for pick in range(picks):
-                here = (tenants[pick] == tenant).astype(F32)
-                total = total + total_ref[pick * RANK : (pick + 1) * RANK, :] * here
-            table_ref[tenant] = total.astype(BF16)
-
-        loop(0, seq_count, table_step)
-
-    build_table(up_sum, up_table)
-    up_back.start()
-    grad_all[me] = finish_column(grad_z, grad_sum, grad_recv)
-    gather_start(grad_gather, grad_share, grad_all)
-    gather_finish(grad_gather, grad_share, grad_all)
+    first_cut, second_cut = planes // 4, 3 * planes // 4
+    loop(0, first_cut, key_step)
+    collect(grad_part, grad_recv, grad_all, grad_move, grad_gather)
+    loop(first_cut, second_cut, key_step)
+    grad_gather.wait_recv()
     down_sum[...] = jnp.zeros_like(down_sum)
 
     def down_step(there):
@@ -562,6 +587,8 @@
     loop(0, planes, down_step)
     build_table(down_sum, down_table)
     down_back.start()
+    loop(second_cut, planes, key_step)
+    pass_on(plane)
 
     members = group // 2
     for column, total, recv_ref, grad in (
@@ -602,6 +629,10 @@
         up_move,
         up_back,
         down_back,
+        low_move,
+        low_gather,
+        grad_move,
+        grad_gather,
     ):
         move.wait_send()
     for source, target, column, share, _ in both:
@@ -616,8 +647,6 @@
             )
         )
     for pair_column, part in (
-        (low_pair_column, low_part),
-        (grad_x, grad_part),
         (key_x, key_out),
         (value_x, value_out),
     ):
@@ -627,24 +656,17 @@
             )
         )
     for column, total in (
-        (low_column, low_sum),
-        (grad_z, grad_sum),
         (key_z, key_mid),
         (value_z, value_mid),
     ):
         column.others(
             lambda there, column=column, total=total: column.sent(total.at[there], there)
         )
-    for column, share, all_ref in (
-        (low_gather, low_share, low_all),
-        (grad_gather, grad_share, grad_all),
-    ):
-        column.others(lambda there, column=column, all_ref=all_ref: column.sent(all_ref.at[me], there))
-        share.every(
-            lambda there, share=share, all_ref=all_ref: share.sent(
-                all_ref.at[2 * there + side], there
-            )
-        )
+
+
+def hand_over_kernel(*refs):
+    for source, target in zip(refs[:5], refs[5:]):
+        target[...] = source[...]
 
 
 def vmem():
@@ -688,10 +710,7 @@
         return jax.ShapeDtypeStruct(dims, dtype)
 
     head_rows = pltpu.VMEM((length, HEAD), BF16)
-    low_plane = pltpu.VMEM((planes, RANK, rows), BF16)
-    low_halves = pltpu.VMEM((planes, 2, RANK, rows), BF16)
     low_blocks = pltpu.VMEM((ctx_count, RANK, rows), BF16)
-    low_buffers = [low_halves, low_plane, low_plane, low_plane, low_blocks]
     key_plane = pltpu.VMEM((planes, rows, HEAD), BF16)
     key_buffers = [pltpu.VMEM((planes, 2, rows, HEAD), BF16), key_plane, key_plane, key_plane]
     attention, key_grad, value_grad, down_grad, up_grad = pl.pallas_call(
@@ -718,17 +737,15 @@
             pltpu.VMEM((stacked, width), BF16),
             pltpu.VMEM((stacked, HEAD), BF16),
             pltpu.VMEM((HEAD, stacked), BF16),
-            *low_buffers,
-            *low_buffers,
+            *[low_blocks] * 6,
             head_rows,
             head_rows,
+            pltpu.VMEM((planes, length, 2 * rows), BF16),
             pltpu.VMEM((planes, length, 2 * rows), BF16),
             pltpu.VMEM((length, 2 * rows), F32),
             pltpu.VMEM((planes, 8, 2 * rows), F32),
             pltpu.VMEM((HEAD, length), BF16),
             pltpu.VMEM((HEAD, length), BF16),
-            pltpu.VMEM((length, HEAD), F32),
-            pltpu.VMEM((length, HEAD), F32),
             *key_buffers,
             *key_buffers,
             pltpu.VMEM((stacked, HEAD), F32),
@@ -737,10 +754,10 @@
             pltpu.VMEM((stacked, width), F32),
             pltpu.VMEM((seq_count, RANK, width), BF16),
             pltpu.VMEM((seq_count, RANK, width), BF16),
-            pltpu.SemaphoreType.DMA((5, ctx_count)),
-            pltpu.SemaphoreType.DMA((5, ctx_count)),
-            pltpu.SemaphoreType.DMA((16, planes)),
-            pltpu.SemaphoreType.DMA((16, planes)),
+            pltpu.SemaphoreType.DMA((9, ctx_count)),
+            pltpu.SemaphoreType.DMA((9, ctx_count)),
+            pltpu.SemaphoreType.DMA((8, planes)),
+            pltpu.SemaphoreType.DMA((8, planes)),
             pltpu.SemaphoreType.DMA((4, seq_count)),
             pltpu.SemaphoreType.DMA((4, seq_count)),
             pltpu.SemaphoreType.DMA((11,)),
@@ -759,6 +776,16 @@
         adapter_up_weight[0],
         sequence_adapter_list,
     )
+    attention, key_grad, value_grad, down_grad, up_grad = pl.pallas_call(
+        hand_over_kernel,
+        name="hand_over",
+        out_shape=tuple(
+            shape(array.shape, array.dtype)
+            for array in (attention, key_grad, value_grad, down_grad, up_grad)
+        ),
+        in_specs=[vmem()] * 5,
+        out_specs=(vmem(),) * 5,
+    )(attention, key_grad, value_grad, down_grad, up_grad)
     return (
         attention[None],
         key_grad[None],

time: 165 us -> 149 us (0.903); the launches traced: 164 us -> 146 us
  Pallas kernels: 156 us -> 143 us
  local copies, waits for them, and re-layouts: 7.93 us -> 2.73 us
    pallas_call x1, Pallas kernels: 156 us -> 141 us  [per_device(): pl.pallas_call(functools.partial(fused_kernel, ctx_count, seq_count, grou...]
    unnamed x20 -> x7, local copies, waits for them, and re-layouts: 7.18 us -> 1.98 us
    pallas_call x0 -> x1, Pallas kernels: none -> 2.23 us  [per_device(): pl.pallas_call(hand_over_kernel, name='hand_over', out_shape=tuple((shape...]
where the time goes in v3:
time: 149 us; the launch traced here: 146 us
  Pallas kernels  143 us (96%)
  local copies, waits for them, and re-layouts  2.73 us (2%)
    pallas_call x1, Pallas kernels, per_device(): pl.pallas_call(functools.partial(fused_kernel, ctx_count, seq_count, grou...  141 us

profile of v3, /device:TPU:1, one launch (start us, length us, event | category | flops | bytes accessed | tf_op | source)
XLA Modules:
  0.0 146.5 jit_solution(14027541037668635932)
XLA Ops:
  0.6 0.0 copy-start.1
  0.6 0.6 copy-done.1
  1.3 0.1 broadcast_in_dim.20
  1.4 0.0 copy-start.2
  1.4 0.1 broadcast_in_dim.21
  1.4 0.6 copy-done.2
  2.0 0.0 copy-start
  2.0 0.6 pad.4.meta
  2.6 0.1 copy-done
  2.7 0.7 copy.15.adapters
  3.4 140.9 %attention_layer.1 = (bf16[128,2048]{1,0:T(8,128)(2,1)}, f32[128,512]{1,0:T(8,128)}, f32[128,512]{1,0:T(8,128)}, f32[64,256]{1,0:T(8,128)}, f32[64,128]{1,0:T(8,128)}) custom-call(bf16[128,4096]{1,0:T(8,128)(2,1)} %bitcast.13, bf16[128,2048]{1,0:T(8,128)(2,1)} %bitcast.14, bf16[128,512]{1,0:T(8,128)(2,1)} %bitcast.16, bf16[128,512]{1,0:T(8,128)(2,1)} %bitcast.17, ...), custom_call_target="tpu_custom_call" | custom-call | tf_op jit(solution)/shard_map/attention_layer/pallas_call | solution.py:716
  144.3 2.2 %hand_over.1 = (bf16[128,2048]{1,0:T(8,128)(2,1)}, f32[128,512]{1,0:T(8,128)}, f32[128,512]{1,0:T(8,128)}, f32[64,256]{1,0:T(8,128)}, f32[64,128]{1,0:T(8,128)}) custom-call(bf16[128,2048]{1,0:T(8,128)(2,1)} %get-tuple-element.15.refs_0_, f32[128,512]{1,0:T(8,128)} %get-tuple-element.16.refs_1_, f32[128,512]{1,0:T(8,128)} %get-tuple-element.17.refs_2_, ...), custom_call_target="tpu_custom_call" | custom-call | tf_op jit(solution)/shard_map/hand_over/pallas_call | solution.py:779
  (1 shorter events, 0.0 us)
Async XLA Ops:
  0.6 0.7 copy-start.1
  1.4 0.7 copy-start.2
  2.0 0.7 copy-start

commit v4 on v3

--- a/solution.py
+++ b/solution.py
@@ -534,6 +534,8 @@
 
     key_x, value_x, key_z, value_z = columns[4:8]
 
+    lag = planes
+
     def key_step(shift):
         there = key_x.away(shift)
         place = aligned(there, block)
@@ -555,9 +557,9 @@
         key_x.to_twin(key_out.at[there, other], key_pair.at[there], there)
         value_x.to_twin(value_out.at[there, other], value_pair.at[there], there)
 
-        @pl.when(shift > 0)
+        @pl.when(shift >= lag)
         def _():
-            pass_on(key_x.away(shift - 1))
+            pass_on(key_x.away(shift - lag))
 
     def pass_on(there):
         for pair_column, column, part, pair, total, recv_ref in (
@@ -573,7 +575,7 @@
             def _():
                 column.to_plane(total.at[there], recv_ref.at[plane], there)
 
-    first_cut, second_cut = planes // 4, 3 * planes // 4
+    first_cut, second_cut = planes // 4, planes
     loop(0, first_cut, key_step)
     collect(grad_part, grad_recv, grad_all, grad_move, grad_gather)
     loop(first_cut, second_cut, key_step)
@@ -588,7 +590,7 @@
     build_table(down_sum, down_table)
     down_back.start()
     loop(second_cut, planes, key_step)
-    pass_on(plane)
+    loop(planes - lag, planes, lambda shift: pass_on(key_x.away(shift)))
 
     members = group // 2
     for column, total, recv_ref, grad in (

time: 149 us -> 142 us (0.953); the launches traced: 146 us -> 141 us
  Pallas kernels: 143 us -> 138 us
    pallas_call x1, Pallas kernels: 141 us -> 136 us  [per_device(): pl.pallas_call(functools.partial(fused_kernel, ctx_count, seq_count, grou...]
where the time goes in v4:
time: 142 us; the launch traced here: 141 us
  Pallas kernels  138 us (97%)
  local copies, waits for them, and re-layouts  2.73 us (2%)
    pallas_call x1, Pallas kernels, per_device(): pl.pallas_call(functools.partial(fused_kernel, ctx_count, seq_count, grou...  136 us

profile of v4, /device:TPU:1, one launch (start us, length us, event | category | flops | bytes accessed | tf_op | source)
XLA Modules:
  0.0 141.5 jit_solution(15857380311704154812)
XLA Ops:
  0.6 0.0 copy-start.1
  0.6 0.6 copy-done.1
  1.3 0.1 broadcast_in_dim.20
  1.4 0.0 copy-start.2
  1.4 0.1 broadcast_in_dim.21
  1.4 0.6 copy-done.2
  2.0 0.0 copy-start
  2.0 0.6 pad.4.meta
  2.6 0.1 copy-done
  2.7 0.7 copy.15.adapters
  3.4 135.8 %attention_layer.1 = (bf16[128,2048]{1,0:T(8,128)(2,1)}, f32[128,512]{1,0:T(8,128)}, f32[128,512]{1,0:T(8,128)}, f32[64,256]{1,0:T(8,128)}, f32[64,128]{1,0:T(8,128)}) custom-call(bf16[128,4096]{1,0:T(8,128)(2,1)} %bitcast.13, bf16[128,2048]{1,0:T(8,128)(2,1)} %bitcast.14, bf16[128,512]{1,0:T(8,128)(2,1)} %bitcast.16, bf16[128,512]{1,0:T(8,128)(2,1)} %bitcast.17, ...), custom_call_target="tpu_custom_call" | custom-call | tf_op jit(solution)/shard_map/attention_layer/pallas_call | solution.py:718
  139.2 2.2 %hand_over.1 = (bf16[128,2048]{1,0:T(8,128)(2,1)}, f32[128,512]{1,0:T(8,128)}, f32[128,512]{1,0:T(8,128)}, f32[64,256]{1,0:T(8,128)}, f32[64,128]{1,0:T(8,128)}) custom-call(bf16[128,2048]{1,0:T(8,128)(2,1)} %get-tuple-element.15.refs_0_, f32[128,512]{1,0:T(8,128)} %get-tuple-element.16.refs_1_, f32[128,512]{1,0:T(8,128)} %get-tuple-element.17.refs_2_, ...), custom_call_target="tpu_custom_call" | custom-call | tf_op jit(solution)/shard_map/hand_over/pallas_call | solution.py:781
  (1 shorter events, 0.0 us)
Async XLA Ops:
  0.6 0.7 copy-start.1
  1.4 0.7 copy-start.2
  2.0 0.7 copy-start

commit v5 on v4

--- a/solution.py
+++ b/solution.py
@@ -14,7 +14,7 @@
 HEAD = 128
 RANK = 64
 TB = 32
-KEY_BLOCK = 512
+KEY_BLOCK = 1024
 MASKED = -1e30
 SCALE = 1.0 / math.sqrt(HEAD)
 LOG2E = math.log2(math.e)

time: 142 us -> 141 us (level)
  no operation moved by 1% of the time
where the time goes in v5:
time: 141 us
  Pallas kernels  137 us (97%)
  local copies, waits for them, and re-layouts  2.73 us (2%)
    pallas_call x1, Pallas kernels, per_device(): pl.pallas_call(functools.partial(fused_kernel, ctx_count, seq_count, grou...  135 us

profile of v5, /device:TPU:1, one launch (start us, length us, event | category | flops | bytes accessed | tf_op | source)
XLA Modules:
  0.0 140.8 jit_solution(6435284202210541158)
XLA Ops:
  0.6 0.0 copy-start.1
  0.6 0.6 copy-done.1
  1.3 0.1 broadcast_in_dim.20
  1.4 0.0 copy-start.2
  1.4 0.1 broadcast_in_dim.21
  1.4 0.6 copy-done.2
  2.0 0.0 copy-start
  2.0 0.6 pad.4.meta
  2.6 0.1 copy-done
  2.7 0.7 copy.15.adapters
  3.4 135.2 %attention_layer.1 = (bf16[128,2048]{1,0:T(8,128)(2,1)}, f32[128,512]{1,0:T(8,128)}, f32[128,512]{1,0:T(8,128)}, f32[64,256]{1,0:T(8,128)}, f32[64,128]{1,0:T(8,128)}) custom-call(bf16[128,4096]{1,0:T(8,128)(2,1)} %bitcast.13, bf16[128,2048]{1,0:T(8,128)(2,1)} %bitcast.14, bf16[128,512]{1,0:T(8,128)(2,1)} %bitcast.16, bf16[128,512]{1,0:T(8,128)(2,1)} %bitcast.17, ...), custom_call_target="tpu_custom_call" | custom-call | tf_op jit(solution)/shard_map/attention_layer/pallas_call | solution.py:718
  138.6 2.2 %hand_over.1 = (bf16[128,2048]{1,0:T(8,128)(2,1)}, f32[128,512]{1,0:T(8,128)}, f32[128,512]{1,0:T(8,128)}, f32[64,256]{1,0:T(8,128)}, f32[64,128]{1,0:T(8,128)}) custom-call(bf16[128,2048]{1,0:T(8,128)(2,1)} %get-tuple-element.15.refs_0_, f32[128,512]{1,0:T(8,128)} %get-tuple-element.16.refs_1_, f32[128,512]{1,0:T(8,128)} %get-tuple-element.17.refs_2_, ...), custom_call_target="tpu_custom_call" | custom-call | tf_op jit(solution)/shard_map/hand_over/pallas_call | solution.py:781
  (1 shorter events, 0.0 us)
Async XLA Ops:
  0.6 0.7 copy-start.1
  1.4 0.7 copy-start.2
  2.0 0.7 copy-start
